TPU v7x, 128 devices: a whole 4x4x4 slice. The times are simulated.
128 devices in a mesh: space: 16 (over y, x_lo, core), filt: 8 (over x_hi, z).
Axes of the slice: x: 4 (x_hi: 2, x_lo: 2; x = x_hi * 2 + x_lo), y: 4, z: 4, core: 2. Of those that a mesh axis runs over, the one named last changes fastest.
Arguments:
- volume: bfloat16 [64, 128, 16, 128], P('space', 'filt'), may hold values from -6 to 6
- w_early: bfloat16 [27, 128, 128], replicated, may hold values from -0.109375 to 0.109375
- w_deep: bfloat16 [27, 128, 256], P(None, None, 'filt'), may hold values from -0.109375 to 0.109375
- cotangent: bfloat16 [32, 64, 8, 256], P('space', None, None, 'filt'), may hold values from -6 to 6
Outputs:
- block_out: bfloat16 [32, 64, 8, 256], P('space', None, None, 'filt')
- grad_early: float32 [27, 128, 128], replicated
- grad_deep: float32 [27, 128, 256], P(None, None, 'filt')
All inputs are finite; a program needn't handle non-finite values.
Results may differ from a plain program's by a relative error of at most 0.0059.
Values may be sent and summed in bfloat16 or wider, within the bound.
A program may use at most 128 MiB of HBM per device.

v0:
```python
import math

import jax
import jax.numpy as jnp
from jax import lax
from jax.sharding import PartitionSpec as P


def extended(block, sides, width):
    for axis, dim in sides:
        count = lax.axis_size(axis)
        forward = [(i, i + 1) for i in range(count - 1)]
        backward = [(target, source) for source, target in forward]
        low = lax.ppermute(
            lax.slice_in_dim(block, block.shape[dim] - width, None, axis=dim), axis, forward
        )
        high = lax.ppermute(lax.slice_in_dim(block, 0, width, axis=dim), axis, backward)
        block = jnp.concatenate([low, block, high], axis=dim)
    return block


def silu_grad(value):
    sig = jax.nn.sigmoid(value)
    return sig * (1.0 + value * (1.0 - sig))


def window(source, tap, size_x, size_y, size_z):
    first = tap // 9
    second = tap // 3 % 3
    third = tap % 3
    part = source[first : first + size_x, second : second + size_y, third : third + size_z]
    return part.reshape(size_x * size_y * size_z, source.shape[3])


def contract_cells(left, right):
    return lax.dot_general(
        left, right, (((0,), (0,)), ((), ())), preferred_element_type=jnp.float32
    )


def shards(volume, w_early, w_deep, cotangent):
    size_x, size_y, size_z, cin = volume.shape
    width = w_early.shape[2]
    cells = size_x * size_y * size_z
    rimmed = extended(volume, (("space", 0), ("filt", 1)), 1)
    padded = jnp.pad(rimmed, ((0, 0), (0, 0), (1, 1), (0, 0)))
    pre_early = jnp.zeros((cells, width), jnp.float32)
    for tap in range(27):
        pre_early = pre_early + jnp.dot(
            window(padded, tap, size_x, size_y, size_z),
            w_early[tap],
            preferred_element_type=jnp.float32,
        )
    pooled = (
        jax.nn.silu(pre_early)
        .reshape(size_x // 2, 2, size_y // 2, 2, size_z // 2, 2, width)
        .mean(axis=(1, 3, 5))
        .astype(jnp.bfloat16)
    )
    local = lax.all_to_all(pooled, "filt", split_axis=3, concat_axis=1, tiled=True)
    half_x, full_y, half_z, shard_c = local.shape
    deep_cells = half_x * full_y * half_z
    filters = w_deep.shape[2]
    slab = extended(local, (("space", 0),), 1)
    slab = jnp.pad(slab, ((0, 0), (1, 1), (1, 1), (0, 0)))

    def kernel_terms(piece):
        return jnp.stack(
            [
                contract_cells(window(piece, tap, half_x, full_y, half_z), grad_pre_deep)
                for tap in range(27)
            ]
        )

    empty = jnp.zeros((deep_cells, filters), jnp.float32)
    total = empty
    piece = lax.all_gather(slab, "filt", axis=3, tiled=True)
    for forward_tap in range(27):
        rows = w_deep[forward_tap]
        total = total + jnp.dot(
            window(piece, forward_tap, half_x, full_y, half_z),
            rows,
            preferred_element_type=jnp.float32,
        )
    block_out = jax.nn.silu(total).astype(jnp.bfloat16).reshape(half_x, full_y, half_z, filters)
    grad_pre_deep = (
        cotangent.reshape(deep_cells, filters).astype(jnp.float32) * silu_grad(total)
    ).astype(jnp.bfloat16)
    deep_terms = kernel_terms(lax.all_gather(slab, "filt", axis=3, tiled=True))
    deep_total = deep_cells * lax.axis_size("space")
    grad_deep = lax.psum(deep_terms, "space") / math.sqrt(deep_total)
    grid_grad = grad_pre_deep.reshape(half_x, full_y, half_z, filters)
    grad_slab = extended(grid_grad, (("space", 0),), 1)
    grad_slab = jnp.pad(grad_slab, ((0, 0), (1, 1), (1, 1), (0, 0)))
    term = jnp.zeros((deep_cells, width), jnp.float32)
    for tap in range(27):
        term = term + jnp.dot(
            window(grad_slab, 26 - tap, half_x, full_y, half_z),
            w_deep[tap].T,
            preferred_element_type=jnp.float32,
        )
    term = term.reshape(half_x, full_y, half_z, width)
    mine = lax.psum_scatter(term, "filt", scatter_dimension=3, tiled=True).astype(jnp.bfloat16)
    grad_pooled = lax.all_to_all(mine, "filt", split_axis=1, concat_axis=3, tiled=True)
    spread = jnp.broadcast_to(
        grad_pooled.astype(jnp.float32)[:, None, :, None, :, None, :],
        (size_x // 2, 2, size_y // 2, 2, size_z // 2, 2, width),
    )
    spread = spread.reshape(cells, width) / 8.0
    grad_pre_early = (spread * silu_grad(pre_early)).astype(jnp.bfloat16)
    early_terms = jnp.stack(
        [
            contract_cells(window(padded, tap, size_x, size_y, size_z), grad_pre_early)
            for tap in range(27)
        ]
    )
    early_total = cells * lax.axis_size("space") * lax.axis_size("filt")
    grad_early = lax.psum(early_terms, ("space", "filt")) / math.sqrt(early_total)
    return (block_out, grad_early, grad_deep)


def solution(mesh):
    return jax.shard_map(
        shards,
        mesh=mesh,
        in_specs=(
            P("space", "filt", None, None),
            P(),
            P(None, None, "filt"),
            P("space", None, None, "filt"),
        ),
        out_specs=(P("space", None, None, "filt"), P(), P(None, None, "filt")),
        check_vma=False,
    )
```

profile of v0, /device:TPU:1, one launch (start us, length us, event | category | flops | bytes accessed | tf_op | source)
XLA Modules:
  0.0 586.7 jit_solution(7086958504121832827)
XLA Ops:
  8.9 4.5 collective-permute-start
  13.4 1.9 collective-permute-start.1
  15.4 3.6 collective-permute-done.1
  19.0 1.3 pad_maximum_fusion.4
  20.4 3.5 collective-permute-start.2
  24.0 1.3 collective-permute-start.3
  25.3 3.4 collective-permute-done.3
  36.6 1.1 fusion.72
  38.9 14.4 %all_to_all.27 = bf16[8,2,1024]{2,1,0:T(2,128)(2,1)S(1)} all-to-all(bf16[8,2,1024]{2,1,0:T(2,128)(2,1)S(1)} %reshape.420), channel_id=1, replica_groups=mesh['space'=16,'filt'=8] {'filt'}, dimensions={0} | all-to-all | bytes 65536 | tf_op jit(solution)/shard_map/all_to_all | solution.py:60
  54.5 2.3 collective-permute-start.5
  56.9 3.7 collective-permute-start.4
  63.2 32.2 %all_gather.4 = bf16[4,66,10,128]{1,0,2,3:T(4,128)(2,1)S(1)} all-gather(bf16[4,66,10,16]{1,0,2,3:T(4,128)(2,1)S(1)} %pad.13.clone), channel_id=1, replica_groups=mesh['space'=16,'filt'=8] {'filt'}, dimensions={3}, use_global_device_ids=true | all-gather | bytes 760320 | tf_op jit(solution)/shard_map/all_gather | solution.py:77
  95.4 5.0 fusion.249
  100.4 12.2 %fusion.248 = (bf16[2,64,8,128]{1,0,2,3:T(2,128)(2,1)}, bf16[2,64,8,128]{1,0,2,3:T(2,128)(2,1)S(1)}, bf16[2,64,8,128]{1,0,2,3:T(2,128)(2,1)}, bf16[2,64,8,128]{1...) fusion(bf16[4,66,10,128]{1,0,2,3:T(4,128)(2,1)S(1)} %all_gather.4), kind=kLoop, calls=%fused_computation.410 | loop fusion | bytes 9961472 | tf_op jit(solution)/shard_map/slice | solution.py:31
  112.6 1.6 copy.200
  114.2 2.2 copy.199
  116.4 2.2 copy.198
  118.7 2.2 copy.197
  120.9 2.3 copy.196
  123.2 2.2 copy.195
  125.4 2.2 copy.194
  127.6 2.2 copy.193
  129.9 2.2 copy.219
  132.6 1.6 copy.217
  134.6 1.6 copy.215
  136.2 1.6 copy.214
  137.7 2.2 copy.213
  140.0 2.2 copy.212
  142.2 2.2 copy.211
  144.4 2.3 copy.210
  146.7 2.2 copy.209
  149.0 2.2 copy.208
  151.2 2.2 copy.207
  153.4 2.2 copy.206
  155.7 2.2 copy.205
  157.9 2.2 copy.204
  160.1 2.4 copy.203
  162.5 2.2 copy.202
  164.8 2.2 copy.201
  167.0 1.2 fusion.192
  168.3 1.2 convolution_add_fusion.71
  169.5 1.2 convolution_add_fusion.70
  170.7 1.2 convolution_add_fusion.69
  179.7 5.4 collective-permute-start.7
  185.1 6.5 %collective-permute-start.6 = (bf16[1,64,8,32]{3,2,1,0:T(8,128)(2,1)}, bf16[1,64,8,32]{3,2,1,0:T(8,128)(2,1)}, u32[]{:S(2)}, u32[]{:S(2)}) collective-permute-start(bf16[1,64,8,32]{3,2,1,0:T(8,128)(2,1)} %bitcast.882), channel_id=1, source_target_pairs={{0,8},{8,16},{16,24},{24,32},{32,40},{40,48},{48,56},{56,64},{64,7... | collective-permute-start | bytes 98312 | tf_op jit(solution)/shard_map/ppermute | solution.py:14
  191.5 1.7 fusion.62
  193.3 1.8 fusion.61
  195.0 1.8 fusion.60
  196.8 1.8 fusion.59
  198.6 1.8 fusion.58
  200.3 1.8 fusion.57
  213.2 1.4 select_maximum_fusion
  216.8 1.1 pad_maximum_fusion.1
  222.2 1.0 convolution_add_fusion
  223.2 2.4 copy.185
  229.5 65.5 %reduce-scatter.2.cloned.1.call-done = f32[2,64,8,16]{1,2,0,3:T(8,128)} async-done(((f32[2,64,8,128]{1,2,0,3:T(8,128)}), f32[2,64,8,16]{1,2,0,3:T(8,128)}) %reduce-scatter.2.cloned.1.call-update) | async-done | bytes 65552 | tf_op jit(solution)/shard_map/reduce_scatter | solution.py:103
  295.0 0.9 convert_element_type.42
  297.1 4.4 all-to-all-start.1
  302.7 5.4 all-to-all-done.1
  321.2 0.9 fusion.23
  335.0 86.9 %all-reduce.8.cloned.1.call-done = f32[27,128,32]{1,2,0:T(8,128)} async-done(((f32[27,128,32]{1,2,0:T(8,128)}), f32[27,128,32]{1,2,0:T(8,128)}) %all-reduce.8.cloned.1.call-update) | async-done | bytes 442384 | tf_op jit(solution)/shard_map/psum | solution.py:91
  421.9 1.8 broadcast_multiply_fusion.1
  423.7 152.3 %all-reduce.6.cloned.1.call-done = f32[27,128,128]{2,1,0:T(8,128)} async-done(((f32[27,128,128]{2,1,0:T(8,128)}), f32[27,128,128]{2,1,0:T(8,128)}) %all-reduce.6.cloned.1.call-update) | async-done | bytes 1769488 | tf_op jit(solution)/shard_map/psum | solution.py:118
  575.9 2.9 broadcast_multiply_fusion
  (334 shorter events, 71.2 us)
Async XLA Ops:
  8.0 287.0 %reduce-scatter.2.cloned.1.call-start = ((), (), s32[]{:S(2)}) async-start(), calls=%async_computation.3 | async-start | bytes 1179648 | tf_op jit(solution)/shard_map/reduce_scatter | solution.py:103
  8.9 6.4 %collective-permute-start = (bf16[1,16,16,128]{3,2,1,0:T(8,128)(2,1)S(1)}, bf16[1,16,16,128]{3,2,1,0:T(8,128)(2,1)S(1)}, u32[]{:S(2)}, u32[]{:S(2)}) collective-permute-start(bf16[1,16,16,128]{3,2,1,0:T(8,128)(2,1)S(1)} %get-tuple-element.112), channel_id=1, source_target_pairs={{0,8},{8,16},{16,24},{24,32},{32,40},{40,48},{48,56},{56,64},{64,7... | collective-permute-start | bytes 196616 | tf_op jit(solution)/shard_map/ppermute | solution.py:14
  13.4 5.6 collective-permute-start.1
  20.4 11.8 %copy-start.37 = (bf16[4,16,16,128]{3,2,1,0:T(8,128)(2,1)}, bf16[4,16,16,128]{3,2,1,0:T(8,128)(2,1)S(1)}, u32[]{:S(2)}) copy-start(bf16[4,16,16,128]{3,2,1,0:T(8,128)(2,1)S(1)} %get-tuple-element.110) | copy-start | bytes 786436
  20.4 15.7 %copy-start.31 = (bf16[4,16,16,128]{3,2,1,0:T(8,128)(2,1)}, bf16[4,16,16,128]{3,2,1,0:T(8,128)(2,1)S(1)}, u32[]{:S(2)}) copy-start(bf16[4,16,16,128]{3,2,1,0:T(8,128)(2,1)S(1)} %get-tuple-element.108) | copy-start | bytes 786436
  20.4 4.9 collective-permute-start.2
  24.0 4.8 collective-permute-start.3
  29.9 3.2 copy-start.51
  29.9 3.6 copy-start.49
  29.9 3.9 copy-start.47
  29.9 4.6 copy-start.45
  29.9 4.8 copy-start.43
  29.9 5.2 copy-start.41
  29.9 5.4 copy-start.39
  30.0 5.9 %copy-start.35 = (bf16[4,16,16,128]{3,2,1,0:T(8,128)(2,1)}, bf16[4,16,16,128]{3,2,1,0:T(8,128)(2,1)S(1)}, u32[]{:S(2)}) copy-start(bf16[4,16,16,128]{3,2,1,0:T(8,128)(2,1)S(1)} %get-tuple-element.77) | copy-start | bytes 786436
  30.0 6.4 %copy-start.33 = (bf16[4,16,16,128]{3,2,1,0:T(8,128)(2,1)}, bf16[4,16,16,128]{3,2,1,0:T(8,128)(2,1)S(1)}, u32[]{:S(2)}) copy-start(bf16[4,16,16,128]{3,2,1,0:T(8,128)(2,1)S(1)} %get-tuple-element.75) | copy-start | bytes 786436
  31.5 3.5 copy-start.55
  31.5 5.1 copy-start.69
  37.9 22.6 %copy-start.77 = (bf16[2,64,8,32]{1,3,2,0:T(8,128)(2,1)S(1)}, bf16[2,64,8,32]{1,3,2,0:T(8,128)(2,1)}, u32[]{:S(2)}) copy-start(bf16[2,64,8,32]{1,3,2,0:T(8,128)(2,1)} %param.7) | copy-start | bytes 196612
  54.5 7.5 %collective-permute-start.5 = (bf16[1,64,8,16]{3,2,1,0:T(8,128)(2,1)S(1)}, bf16[1,64,8,16]{3,2,1,0:T(8,128)(2,1)S(1)}, u32[]{:S(2)}, u32[]{:S(2)}) collective-permute-start(bf16[1,64,8,16]{3,2,1,0:T(8,128)(2,1)S(1)} %bitcast.885), channel_id=1, source_target_pairs={{8,0},{16,8},{24,16},{32,24},{40,32},{48,40},{56,48},{64,56},{72,6... | collective-permute-start | bytes 49160 | tf_op jit(solution)/shard_map/ppermute | solution.py:17
  56.9 5.6 collective-permute-start.4
  167.0 4.8 copy-start.13
  167.0 4.9 copy-start.73
  167.0 5.1 copy-start.10
  167.0 5.3 copy-start.7
  168.2 4.5 copy-start.29
  169.5 3.5 copy-start.26
  179.7 23.2 %copy-start.30 = (bf16[2,64,8,128]{3,2,1,0:T(8,128)(2,1)S(1)}, bf16[2,64,8,128]{3,2,1,0:T(8,128)(2,1)}, u32[]{:S(2)}) copy-start(bf16[2,64,8,128]{3,2,1,0:T(8,128)(2,1)} %copy.201) | copy-start | bytes 786436
  179.7 24.0 %copy-start.27 = (bf16[2,64,8,128]{3,2,1,0:T(8,128)(2,1)S(1)}, bf16[2,64,8,128]{3,2,1,0:T(8,128)(2,1)}, u32[]{:S(2)}) copy-start(bf16[2,64,8,128]{3,2,1,0:T(8,128)(2,1)} %copy.202) | copy-start | bytes 786436
  179.7 24.8 %copy-start.25 = (bf16[2,64,8,128]{3,2,1,0:T(8,128)(2,1)S(1)}, bf16[2,64,8,128]{3,2,1,0:T(8,128)(2,1)}, u32[]{:S(2)}) copy-start(bf16[2,64,8,128]{3,2,1,0:T(8,128)(2,1)} %copy.203) | copy-start | bytes 786436
  179.7 25.5 %copy-start.23 = (bf16[2,64,8,128]{3,2,1,0:T(8,128)(2,1)S(1)}, bf16[2,64,8,128]{3,2,1,0:T(8,128)(2,1)}, u32[]{:S(2)}) copy-start(bf16[2,64,8,128]{3,2,1,0:T(8,128)(2,1)} %copy.204) | copy-start | bytes 786436
  179.7 33.5 %collective-permute-start.7 = (bf16[1,64,8,32]{3,2,1,0:T(8,128)(2,1)}, bf16[1,64,8,32]{3,2,1,0:T(8,128)(2,1)}, u32[]{:S(2)}, u32[]{:S(2)}) collective-permute-start(bf16[1,64,8,32]{3,2,1,0:T(8,128)(2,1)} %bitcast.883), channel_id=1, source_target_pairs={{8,0},{16,8},{24,16},{32,24},{40,32},{48,40},{56,48},{64,56},{72,6... | collective-permute-start | bytes 98312 | tf_op jit(solution)/shard_map/ppermute | solution.py:17
  185.1 28.1 %collective-permute-start.6 = (bf16[1,64,8,32]{3,2,1,0:T(8,128)(2,1)}, bf16[1,64,8,32]{3,2,1,0:T(8,128)(2,1)}, u32[]{:S(2)}, u32[]{:S(2)}) collective-permute-start(bf16[1,64,8,32]{3,2,1,0:T(8,128)(2,1)} %bitcast.882), channel_id=1, source_target_pairs={{0,8},{8,16},{16,24},{24,32},{32,40},{40,48},{48,56},{56,64},{64,7... | collective-permute-start | bytes 98312 | tf_op jit(solution)/shard_map/ppermute | solution.py:14
  193.3 12.7 %copy-start.21 = (bf16[2,64,8,128]{3,2,1,0:T(8,128)(2,1)S(1)}, bf16[2,64,8,128]{3,2,1,0:T(8,128)(2,1)}, u32[]{:S(2)}) copy-start(bf16[2,64,8,128]{3,2,1,0:T(8,128)(2,1)} %copy.205) | copy-start | bytes 786436
  195.0 11.8 %copy-start.19 = (bf16[2,64,8,128]{3,2,1,0:T(8,128)(2,1)S(1)}, bf16[2,64,8,128]{3,2,1,0:T(8,128)(2,1)}, u32[]{:S(2)}) copy-start(bf16[2,64,8,128]{3,2,1,0:T(8,128)(2,1)} %copy.206) | copy-start | bytes 786436
  196.8 10.8 %copy-start.17 = (bf16[2,64,8,128]{3,2,1,0:T(8,128)(2,1)S(1)}, bf16[2,64,8,128]{3,2,1,0:T(8,128)(2,1)}, u32[]{:S(2)}) copy-start(bf16[2,64,8,128]{3,2,1,0:T(8,128)(2,1)} %copy.207) | copy-start | bytes 786436
  198.6 9.8 %copy-start.15 = (bf16[2,64,8,128]{3,2,1,0:T(8,128)(2,1)S(1)}, bf16[2,64,8,128]{3,2,1,0:T(8,128)(2,1)}, u32[]{:S(2)}) copy-start(bf16[2,64,8,128]{3,2,1,0:T(8,128)(2,1)} %copy.208) | copy-start | bytes 786436
  200.3 8.8 %copy-start.12 = (bf16[2,64,8,128]{3,2,1,0:T(8,128)(2,1)S(1)}, bf16[2,64,8,128]{3,2,1,0:T(8,128)(2,1)}, u32[]{:S(2)}) copy-start(bf16[2,64,8,128]{3,2,1,0:T(8,128)(2,1)} %copy.209) | copy-start | bytes 786436
  202.1 7.8 %copy-start.9 = (bf16[2,64,8,128]{3,2,1,0:T(8,128)(2,1)S(1)}, bf16[2,64,8,128]{3,2,1,0:T(8,128)(2,1)}, u32[]{:S(2)}) copy-start(bf16[2,64,8,128]{3,2,1,0:T(8,128)(2,1)} %copy.210) | copy-start | bytes 786436
  202.9 7.8 %copy-start.6 = (bf16[2,64,8,128]{3,2,1,0:T(8,128)(2,1)S(1)}, bf16[2,64,8,128]{3,2,1,0:T(8,128)(2,1)}, u32[]{:S(2)}) copy-start(bf16[2,64,8,128]{3,2,1,0:T(8,128)(2,1)} %copy.211) | copy-start | bytes 786436
  203.7 7.8 %copy-start.4 = (bf16[2,64,8,128]{3,2,1,0:T(8,128)(2,1)S(1)}, bf16[2,64,8,128]{3,2,1,0:T(8,128)(2,1)}, u32[]{:S(2)}) copy-start(bf16[2,64,8,128]{3,2,1,0:T(8,128)(2,1)} %copy.212) | copy-start | bytes 786436
  204.4 7.8 %copy-start.2 = (bf16[2,64,8,128]{3,2,1,0:T(8,128)(2,1)S(1)}, bf16[2,64,8,128]{3,2,1,0:T(8,128)(2,1)}, u32[]{:S(2)}) copy-start(bf16[2,64,8,128]{3,2,1,0:T(8,128)(2,1)} %copy.213) | copy-start | bytes 786436
  225.6 75.9 %copy-start.72 = (bf16[2,64,8,128]{3,2,1,0:T(8,128)(2,1)S(1)}, bf16[2,64,8,128]{3,2,1,0:T(8,128)(2,1)}, u32[]{:S(2)}) copy-start(bf16[2,64,8,128]{3,2,1,0:T(8,128)(2,1)} %copy.219) | copy-start | bytes 786436
  297.1 11.0 %all-to-all-start.1 = ((bf16[8,2,1024]{2,1,0:T(2,128)(2,1)}), bf16[8,2,1024]{2,1,0:T(2,128)(2,1)S(1)}, u32[]{:S(2)}, u32[]{:S(2)}) async-start(bf16[8,2,1024]{2,1,0:T(2,128)(2,1)} %reshape.422), calls=%async_computation.2 | async-start | bytes 65536 | tf_op jit(solution)/shard_map/all_to_all | solution.py:104
  301.5 120.4 %all-reduce.8.cloned.1.call-start = ((), (), s32[]{:S(2)}) async-start(), calls=%async_computation.5 | async-start | bytes 884736 | tf_op jit(solution)/shard_map/psum | solution.py:91
  302.3 6.8 %copy-start.76 = (f32[1024,128]{1,0:T(8,128)S(1)}, f32[1024,128]{1,0:T(8,128)}, u32[]{:S(2)}) copy-start(f32[1024,128]{1,0:T(8,128)} %get-tuple-element.118) | copy-start | bytes 1572868
  302.4 273.6 %all-reduce.6.cloned.1.call-start = ((), (), s32[]{:S(2)}) async-start(), calls=%async_computation.4 | async-start | bytes 3538944 | tf_op jit(solution)/shard_map/psum | solution.py:118
  309.1 3.9 copy-start.38
  309.3 5.5 copy-start.58
  310.3 5.5 copy-start.66
  311.2 5.5 copy-start.54
  312.1 5.4 copy-start.52
  313.0 5.4 copy-start.64
  313.9 5.4 copy-start.50
  314.8 5.4 copy-start.48
  316.6 5.4 copy-start.46
  317.5 5.4 copy-start.44
  318.4 5.4 copy-start.56
  319.3 5.4 copy-start.42
  320.2 5.5 copy-start.40
  323.0 5.5 copy-start.36
  323.9 5.5 copy-start.32
  325.7 5.5 copy-start.34
  326.6 5.5 copy-start.70
  (28 other events, 48.4 us)
Sparse Core Ops, SparseCore 0:
  225.7 69.1 reduce-scatter.1
Sparse Core Ops, SparseCore 1:
  305.0 116.8 all-reduce.7
  427.1 148.8 all-reduce.5
where the time goes:
time: 595 us; the launch traced here: 587 us
  waiting for transfers between devices  318 us (53%)
  local copies, waits for them, and re-layouts  87 us (15%)
  matrix products  73.5 us (12%)
  blocking collectives  46.6 us (8%)
  starting transfers between devices  33.9 us (6%)
  between operations  17.5 us (3%)
  other arithmetic  10.6 us (2%)
    psum x1, waiting for transfers between devices, shards(): lax.psum(early_terms, ('space', 'filt')) / math.sqrt(early_total)  152 us
    psum x1, waiting for transfers between devices, shards(): grad_deep = lax.psum(deep_terms, 'space') / math.sqrt(deep_total)  86.9 us
    reduce_scatter x1, waiting for transfers between devices, shards(): lax.psum_scatter(term, 'filt', scatter_dimension=3, tiled=True)  65.5 us
    unnamed x194, local copies, waits for them, and re-layouts  59.2 us
    dot_general x54, matrix products, contract_cells(): lax.dot_general(left, right, (((0,), (0,)), ((), ())), preferred_element_...  51.3 us
    all_gather x1, blocking collectives, shards(): piece = lax.all_gather(slab, 'filt', axis=3, tiled=True)  32.2 us
    slice x5, local copies, waits for them, and re-layouts, window(): source[first:first + size_x, second:second + size_y, third:third + size_z]  19 us
    ppermute x4, starting transfers between devices, extended(): lax.ppermute(lax.slice_in_dim(block, block.shape[dim] - width, None, axis...  18.2 us
  transfers between devices with their start and end apart: 12, of which 7 were waited for; matrix products, arithmetic and copies ran while one was open for 10% of the time, Pallas kernels for 0%

commit v1 on v0

v1 whole, which is shorter than its diff:
```python
import functools
import math

import jax
import jax.numpy as jnp
from jax import lax
from jax.experimental import pallas as pl
from jax.experimental.pallas import tpu as pltpu
from jax.sharding import PartitionSpec as P

MESH = pl.DeviceIdType.MESH
BF = jnp.bfloat16
F32 = jnp.float32
SPACE, FILT, CHIPS = 16, 8, 64
DIRS = [(ds, df) for ds in (-1, 0, 1) for df in (-1, 0, 1) if ds or df]
GROUP = 4
OWNERS = 7


def rcopy(src, dst, send_sem, recv_sem, device):
    return pltpu.make_async_remote_copy(
        src_ref=src,
        dst_ref=dst,
        send_sem=send_sem,
        recv_sem=recv_sem,
        device_id=device,
        device_id_type=MESH,
    )


def sigmoid(v):
    return 1.0 / (1.0 + jnp.exp(-v))


def shift_rows(v, step):
    size = v.shape[1]
    row = lax.broadcasted_iota(jnp.int32, v.shape, 1)
    edge = size - 1 if step == 1 else 0
    rolled = pltpu.roll(v, (-step) % size, 1)
    return jnp.where(row == edge, 0.0, rolled)


def dot(a, b):
    return lax.dot_general(a, b, (((1,), (0,)), ((), ())), preferred_element_type=F32)


def dot_t(a, b):
    return lax.dot_general(a, b, (((1,), (1,)), ((), ())), preferred_element_type=F32)


def edges(step, size):
    if step == 1:
        return size - 1, 0, 1
    if step == -1:
        return 0, size + 1, 1
    return 0, 1, size


class Halo:
    def __init__(self, source, base, padded, nx, ny, sems, s, f):
        self.items = []
        for k, (ds, df) in enumerate(DIRS):
            sx, dx, lx = edges(ds, nx)
            sy, dy, ly = edges(df, ny)
            src = source.at[base + sx : base + sx + lx, base + sy : base + sy + ly]
            dst = padded.at[dx : dx + lx, dy : dy + ly]
            to_s, to_f, from_s, from_f = s + ds, f + df, s - ds, f - df
            send = (to_s >= 0) & (to_s < SPACE) & (to_f >= 0) & (to_f < FILT)
            recv = (from_s >= 0) & (from_s < SPACE) & (from_f >= 0) & (from_f < FILT)
            copy = rcopy(src, dst, sems.at[0, k], sems.at[1, k], (to_s, to_f))
            self.items.append((copy, send, recv))

    def start(self):
        for copy, send, _ in self.items:
            pl.when(send)(copy.start)

    def wait_recv(self):
        for copy, _, recv in self.items:
            pl.when(recv)(copy.wait_recv)

    def wait_send(self):
        for copy, send, _ in self.items:
            pl.when(send)(copy.wait_send)


def zero_rim(padded, nx, ny, s, f):
    shape = padded.shape

    @pl.when(s == 0)
    def _():
        padded[0:1] = jnp.zeros((1,) + shape[1:], padded.dtype)

    @pl.when(s == SPACE - 1)
    def _():
        padded[nx + 1 : nx + 2] = jnp.zeros((1,) + shape[1:], padded.dtype)

    @pl.when(f == 0)
    def _():
        padded[:, 0:1] = jnp.zeros((shape[0], 1) + shape[2:], padded.dtype)

    @pl.when(f == FILT - 1)
    def _():
        padded[:, ny + 1 : ny + 2] = jnp.zeros((shape[0], 1) + shape[2:], padded.dtype)


SCRATCH = dict(
    vp=((6, 18, 16, 128), BF),
    zc=((6, 18, 16, 384), BF),
    we=((9, 384, 128), BF),
    wd=((27, 128, 32), BF),
    ct=((2, 64, 8, 32), BF),
    wg=((9, 256, 384), BF),
    cs=((8, 2, 16, 128), BF),
    cr=((2, 8, 16, 128), BF),
    acc=((1024, 128), F32),
    sg=((4, 16, 16, 128), F32),
    tmp=((16, 16, 128), F32),
    pp=((4, 10, 8, 128), BF),
    pz=((4, 10, 8, 384), F32),
    ps=((2, 66, 8, 128), BF),
    ps3=((2, 66, 8, 384), F32),
    bs=((2, 8, 16, 128), BF),
    br=((8, 2, 16, 128), BF),
    gp=((4, 10, 8, 256), BF),
    gf=((4, 10, 8, 256), F32),
    gs=((2, 3, 8, 16, 128), BF),
    gr=((2, 3, 16, 1024), BF),
    gt=((128, 1024), BF),
    xs=((9, 64, 384), BF),
    xr=((9, 64, 384), BF),
    xo=((9, 64, 384), F32),
    es=((8, 28, 8, 128), BF),
    er=((64, 4, 8, 128), BF),
    ea=((2, 8, 28, 8, 128), BF),
    pb=((1024, 1152), BF),
    hs=((48, 1152), BF),
    hr=((48, 1152), BF),
    ho=((48, 1152), F32),
    dsd=((28, 16, 128), BF),
    dr=((8, 4, 16, 128), BF),
    da=((2, 28, 16, 128), BF),
)
SEMS = dict(
    local=(3,),
    halo_v=(2, 8),
    halo_p=(2, 8),
    halo_g=(2, 8),
    s_cot=(2, 8),
    s_wg=(2, 8),
    s_wrel=(2,),
    s_ps=(2, 8),
    s_bo=(2, 8),
    s_g=(2, 8),
    s_x=(2, 9),
    s_rs=(2, 64),
    s_ag=(2, 64),
    s_ear=(2,),
    s_h=(2,),
    s_drs=(2, 8),
    s_dag=(2, 8),
    s_dar=(2,),
)


def kernel(early_scale, deep_scale, vol, we_in, wd_in, ct_in, bo_out, ge_out, gd_out, *scratch):
    r = dict(zip(list(SCRATCH) + list(SEMS), scratch))
    s = lax.axis_index("space")
    f = lax.axis_index("filt")
    core = lax.rem(s, 2)
    other = 1 - core
    sib = s + 1 - 2 * core
    j = lax.div(s, 2)

    def filt_peer(k):
        return lax.rem(f + k, FILT)

    def filt_from(k):
        return lax.rem(f + FILT - k, FILT)

    def chip(k):
        dj, df = lax.div(k, 8), lax.rem(k, 8)
        return lax.rem(s + 2 * dj, SPACE), lax.rem(f + df, FILT)

    def chip_from(k):
        dj, df = lax.div(k, 8), lax.rem(k, 8)
        return lax.rem(s + SPACE - 2 * dj, SPACE), lax.rem(f + FILT - df, FILT)

    barrier = pltpu.get_barrier_semaphore()

    def greet(k, carry):
        pl.semaphore_signal(barrier, inc=1, device_id=chip(k), device_id_type=MESH)
        return carry

    for d in (1, SPACE - 1):
        for df in (0, 1, FILT - 1):
            pl.semaphore_signal(
                barrier,
                inc=1,
                device_id=(lax.rem(s + d, SPACE), lax.rem(f + df, FILT)),
                device_id_type=MESH,
            )
    lax.fori_loop(1, CHIPS, greet, 0)

    own_vol = pltpu.make_async_copy(vol, r["vp"].at[1:5, 1:17], r["local"].at[0])
    own_vol.start()
    own_wd = pltpu.make_async_copy(wd_in, r["wd"], r["local"].at[1])
    own_wd.start()
    own_ct = pltpu.make_async_copy(ct_in, r["ct"], r["local"].at[2])
    own_ct.start()
    own_wd.wait()
    wg = r["wg"]
    for t in range(27):
        wt = r["wd"][t].astype(F32).T.astype(BF)
        lanes = slice(128 * (t % 3), 128 * (t % 3) + 128)
        for h in range(2):

            @pl.when(core == h)
            def _():
                rows = pl.ds(pl.multiple_of(128 * h + 16 * f, 16), 16)
                wg[t // 3, rows, lanes] = wt[16 * h : 16 * h + 16]

    own_ct.wait()
    for q in range(8):
        piece = r["ct"][:, 8 * q : 8 * q + 8].astype(F32).reshape(128, 32)
        r["cs"][q] = piece.T.astype(BF).reshape(2, 16, 128)
    zero_rim(r["vp"], 4, 16, s, f)
    zero_rim(r["pp"], 2, 8, s, f)
    zero_rim(r["gp"], 2, 8, s, f)
    r["ps"][:, 0:1] = jnp.zeros((2, 1, 8, 128), BF)
    r["ps"][:, 65:66] = jnp.zeros((2, 1, 8, 128), BF)

    pl.semaphore_wait(barrier, CHIPS - 1 + 6)
    halo_v = Halo(vol, 0, r["vp"], 4, 16, r["halo_v"], s, f)
    halo_v.start()
    own_we = pltpu.make_async_copy(we_in, r["we"], r["local"].at[1])
    own_we.start()

    cots = []
    for k in range(1, FILT):
        cots.append(
            rcopy(
                r["cs"].at[filt_peer(k)],
                r["cr"].at[:, f],
                r["s_cot"].at[0, k],
                r["s_cot"].at[1, k],
                (s, filt_peer(k)),
            )
        )
        cots[-1].start()
    wgs = []
    for k in range(1, FILT):
        rows = pl.ds(pl.multiple_of(128 * core + 16 * f, 16), 16)
        wgs.append(
            rcopy(
                wg.at[:, rows],
                wg.at[:, rows],
                r["s_wg"].at[0, k],
                r["s_wg"].at[1, k],
                (s, filt_peer(k)),
            )
        )
        wgs[-1].start()
    r["cr"][:, pl.ds(f, 1)] = r["cs"][pl.ds(f, 1)].reshape(2, 1, 16, 128)

    own_vol.wait()
    halo_v.wait_recv()
    zc = r["zc"]
    for row in range(6):
        x = r["vp"][row].astype(F32)
        zc[row, :, :, 0:128] = shift_rows(x, -1).astype(BF)
        zc[row, :, :, 128:256] = r["vp"][row]
        zc[row, :, :, 256:384] = shift_rows(x, 1).astype(BF)
    own_we.wait()
    acc = r["acc"]
    for ab in range(9):
        a, b = ab // 3, ab % 3
        patch = zc[a : a + 4, b : b + 16].reshape(1024, 384)
        term = dot(patch, r["we"][ab])
        if ab == 0:
            acc[...] = term
        else:
            acc[...] += term
    for half in range(2):
        v = acc[512 * half : 512 * half + 512].reshape(2, 16, 16, 128)
        sig = sigmoid(v)
        r["sg"][2 * half : 2 * half + 2] = sig * (1.0 + v * (1.0 - sig)) * 0.125
        act = v * sig
        act = (act[0] + act[1]).reshape(8, 2, 16, 128)
        r["tmp"][8 * half : 8 * half + 8] = act[:, 0] + act[:, 1]
    tmp = r["tmp"]
    pooled = (tmp[:, pl.ds(0, 8, stride=2), :] + tmp[:, pl.ds(1, 8, stride=2), :]) * 0.125
    pooled = pooled.reshape(2, 8, 8, 128).astype(BF)
    r["pp"][1:3, 1:9] = pooled
    halo_p = Halo(r["pp"], 1, r["pp"], 2, 8, r["halo_p"], s, f)
    halo_p.start()
    pss = []
    for k in range(1, FILT):
        pss.append(
            rcopy(
                r["pp"].at[1:3, 1:9],
                r["ps"].at[:, pl.ds(1 + 8 * f, 8)],
                r["s_ps"].at[0, k],
                r["s_ps"].at[1, k],
                (s, filt_peer(k)),
            )
        )
        pss[-1].start()
    r["ps"][:, pl.ds(1 + 8 * f, 8)] = pooled

    for c in wgs:
        c.wait_recv()
    mine = pl.ds(pl.multiple_of(128 * core, 128), 128)
    wrel = rcopy(wg.at[:, mine], wg.at[:, mine], r["s_wrel"].at[0], r["s_wrel"].at[1], (sib, f))
    wrel.start()
    for c in cots:
        c.wait_recv()
    cot = r["cr"][...].reshape(256, 128).astype(F32).T
    halo_p.wait_recv()
    pz = r["pz"]
    for row in range(4):
        x = r["pp"][row].astype(F32)
        pz[row, :, :, 0:128] = shift_rows(x, -1)
        pz[row, :, :, 128:256] = x
        pz[row, :, :, 256:384] = shift_rows(x, 1)
    wrel.wait_recv()

    pre = jnp.zeros((128, 256), F32)
    for ab in range(9):
        a, b = ab // 3, ab % 3
        patch = pz[a : a + 2, b : b + 8].reshape(128, 384).astype(BF)
        pre = pre + dot_t(patch, wg[ab])
    sig = sigmoid(pre)
    g = (cot * (sig * (1.0 + pre * (1.0 - sig)))).astype(BF)
    r["gp"][1:3, 1:9] = g.astype(F32).reshape(2, 8, 8, 256).astype(BF)
    halo_g = Halo(r["gp"], 1, r["gp"], 2, 8, r["halo_g"], s, f)
    halo_g.start()
    r["bs"][...] = (pre * sig).T.astype(BF).reshape(2, 8, 16, 128)
    bos = []
    for k in range(1, FILT):
        bos.append(
            rcopy(
                r["bs"].at[:, filt_peer(k)],
                r["br"].at[f],
                r["s_bo"].at[0, k],
                r["s_bo"].at[1, k],
                (s, filt_peer(k)),
            )
        )
        bos[-1].start()
    r["br"][pl.ds(f, 1)] = r["bs"][:, pl.ds(f, 1)].reshape(1, 2, 16, 128)

    halo_g.wait_recv()
    gf = r["gf"]
    gf[...] = r["gp"][...].astype(F32)
    back = jnp.zeros((128, 384), F32)
    for ab in range(9):
        a, b = ab // 3, ab % 3
        patch = gf[2 - a : 4 - a, 2 - b : 10 - b].reshape(128, 256).astype(BF)
        back = back + dot(patch, wg[ab])
    back = back.reshape(16, 8, 384)
    gpool = (
        shift_rows(back[:, :, 0:128], 1)
        + back[:, :, 128:256]
        + shift_rows(back[:, :, 256:384], -1)
    )
    gpool = gpool.astype(BF).astype(F32)
    tmp[:, pl.ds(0, 8, stride=2), :] = gpool
    tmp[:, pl.ds(1, 8, stride=2), :] = gpool
    for row in range(4):
        spread = tmp[8 * (row // 2) : 8 * (row // 2) + 8]
        spread = jnp.broadcast_to(spread[:, None], (8, 2, 16, 128)).reshape(16, 16, 128)
        grad = (spread * r["sg"][row]).astype(BF).astype(F32).reshape(256, 128)
        r["gt"][:, 256 * row : 256 * row + 256] = grad.T.astype(BF)

    gt = r["gt"][...]
    xcs = []
    for ab in range(9):
        a, b = ab // 3, ab % 3
        term = dot(gt, zc[a : a + 4, b : b + 16].reshape(1024, 384))

        @pl.when(core == 0)
        def _():
            r["xo"][ab] = term[0:64]
            r["xs"][ab] = term[64:128].astype(BF)

        @pl.when(core == 1)
        def _():
            r["xo"][ab] = term[64:128]
            r["xs"][ab] = term[0:64].astype(BF)

        xcs.append(
            rcopy(r["xs"].at[ab], r["xr"].at[ab], r["s_x"].at[0, ab], r["s_x"].at[1, ab], (sib, f))
        )
        xcs[-1].start()

    for a in range(3):
        piece = gf[2 - a : 4 - a, 1:9].reshape(128, 256)
        r["gs"][:, a] = piece.T.astype(BF).reshape(2, 8, 16, 128)
    gcs = []
    lanes = pl.ds(pl.multiple_of(128 * f, 128), 128)
    for k in range(1, FILT):
        gcs.append(
            rcopy(
                r["gs"].at[:, :, filt_peer(k)],
                r["gr"].at[:, :, :, lanes],
                r["s_g"].at[0, k],
                r["s_g"].at[1, k],
                (s, filt_peer(k)),
            )
        )
        gcs[-1].start()
    r["gr"][:, :, :, lanes] = r["gs"][:, :, pl.ds(f, 1)].reshape(2, 3, 16, 128)

    es = r["es"]
    es[:, 27:28] = jnp.zeros((8, 1, 8, 128), BF)
    for ab in range(9):
        xcs[ab].wait_recv()
        total = r["xo"][ab] + r["xr"][ab].astype(F32)
        for c in range(3):
            es[:, 3 * ab + c] = total[:, 128 * c : 128 * c + 128].reshape(8, 8, 128).astype(BF)

    er = r["er"]

    def rs_copy(k):
        to_s, to_f = chip(k)
        to_j = lax.div(to_s, 2)
        first = jnp.minimum(GROUP * to_j, GROUP * (OWNERS - 1))
        copy = rcopy(
            es.at[to_f, pl.ds(first, GROUP)],
            er.at[k],
            r["s_rs"].at[0, k],
            r["s_rs"].at[1, k],
            (to_s, to_f),
        )
        return copy, to_j < OWNERS

    def rs_start(k, carry):
        copy, active = rs_copy(k)
        pl.when(active)(copy.start)
        return carry

    lax.fori_loop(1, CHIPS, rs_start, 0)

    for c in pss:
        c.wait_recv()
    ps3 = r["ps3"]
    for row in range(2):
        x = r["ps"][row].astype(F32)
        ps3[row, :, :, 0:128] = shift_rows(x, -1)
        ps3[row, :, :, 128:256] = x
        ps3[row, :, :, 256:384] = shift_rows(x, 1)
    for q in range(8):
        for b in range(3):
            patch = ps3[:, 8 * q + b : 8 * q + b + 8].reshape(128, 384).astype(BF)
            r["pb"][128 * q : 128 * q + 128, 384 * b : 384 * b + 384] = patch
    for c in gcs:
        c.wait_recv()
    deep = dot(r["gr"][...].reshape(96, 1024), r["pb"][...])

    @pl.when(core == 0)
    def _():
        r["ho"][...] = deep[0:48]
        r["hs"][...] = deep[48:96].astype(BF)

    @pl.when(core == 1)
    def _():
        r["ho"][...] = deep[48:96]
        r["hs"][...] = deep[0:48].astype(BF)

    hcopy = rcopy(r["hs"], r["hr"], r["s_h"].at[0], r["s_h"].at[1], (sib, f))
    hcopy.start()

    for c in bos:
        c.wait_recv()
    for q in range(8):
        piece = r["br"][q].reshape(32, 128).astype(F32).T
        bo_out[:, 8 * q : 8 * q + 8] = piece.reshape(2, 8, 8, 32).astype(BF)

    hcopy.wait_recv()
    dsd = r["dsd"]
    dsd[27:28] = jnp.zeros((1, 16, 128), BF)
    total = r["ho"][...] + r["hr"][...].astype(F32)
    for a in range(3):
        for bc in range(9):
            dsd[9 * a + bc] = total[16 * a : 16 * a + 16, 128 * bc : 128 * bc + 128].astype(BF)

    def space_chip(k):
        return lax.rem(s + 2 * k, SPACE)

    def first_of(jj):
        return jnp.minimum(GROUP * jj, GROUP * (OWNERS - 1))

    drs = []
    for k in range(1, 8):
        to_s = space_chip(k)
        to_j = lax.div(to_s, 2)
        copy = rcopy(
            dsd.at[pl.ds(first_of(to_j), GROUP)],
            r["dr"].at[k],
            r["s_drs"].at[0, k],
            r["s_drs"].at[1, k],
            (to_s, f),
        )
        pl.when(to_j < OWNERS)(copy.start)
        drs.append((copy, to_j < OWNERS))

    mine_t = pl.ds(first_of(j), GROUP)
    owner = j < OWNERS

    def rs_wait(k, carry):
        copy, _ = rs_copy(k)
        copy.wait_recv()
        return carry

    ea = r["ea"]

    def ag_copy(k):
        to_s, to_f = chip(k)
        piece = ea.at[core, f, mine_t]
        return rcopy(piece, piece, r["s_ag"].at[0, k], r["s_ag"].at[1, k], (to_s, to_f))

    @pl.when(owner)
    def _():
        lax.fori_loop(1, CHIPS, rs_wait, 0)
        total = es[pl.ds(f, 1), mine_t].reshape(GROUP, 8, 128).astype(F32)

        def add(k, total):
            return total + er[k].astype(F32)

        total = lax.fori_loop(1, CHIPS, add, total)
        total = (total * early_scale).astype(BF).reshape(1, 1, GROUP, 8, 128)
        ea[pl.ds(core, 1), pl.ds(f, 1), mine_t] = total

        def ag_start(k, carry):
            ag_copy(k).start()
            return carry

        lax.fori_loop(1, CHIPS, ag_start, 0)

    da = r["da"]
    piece = da.at[core, mine_t]
    dag = []
    for k in range(1, 8):
        dag.append(
            rcopy(piece, piece, r["s_dag"].at[0, k], r["s_dag"].at[1, k], (space_chip(k), f))
        )

    @pl.when(owner)
    def _():
        total = dsd[mine_t].astype(F32)
        for k in range(1, 8):
            drs[k - 1][0].wait_recv()
            total = total + r["dr"][k].astype(F32)
        da[pl.ds(core, 1), mine_t] = (total * deep_scale).astype(BF).reshape(1, GROUP, 16, 128)
        for c in dag:
            c.start()

    for k in range(1, 8):
        from_j = lax.div(lax.rem(s + SPACE - 2 * k, SPACE), 2)
        pl.when(from_j < OWNERS)(dag[k - 1].wait_recv)
    dar = rcopy(da.at[core], da.at[core], r["s_dar"].at[0], r["s_dar"].at[1], (sib, f))
    dar.start()

    def ag_wait(k, carry):
        from_s, _ = chip_from(k)
        pl.when(lax.div(from_s, 2) < OWNERS)(ag_copy(k).wait_recv)
        return carry

    lax.fori_loop(1, CHIPS, ag_wait, 0)
    ear = rcopy(ea.at[core], ea.at[core], r["s_ear"].at[0], r["s_ear"].at[1], (sib, f))
    ear.start()

    dar.wait_recv()
    for t in range(27):
        gd_out[t] = da[:, t].reshape(32, 128).astype(F32).T
    ear.wait_recv()
    for t in range(27):
        ge_out[t] = ea[:, :, t].astype(F32).reshape(128, 128).T

    for h in (halo_v, halo_p, halo_g):
        h.wait_send()
    for c in cots + wgs + pss + bos + gcs + xcs + [wrel, hcopy, dar, ear]:
        c.wait_send()
    for copy, active in drs:
        pl.when(active)(copy.wait_send)

    def rs_sent(k, carry):
        copy, active = rs_copy(k)
        pl.when(active)(copy.wait_send)
        return carry

    lax.fori_loop(1, CHIPS, rs_sent, 0)

    @pl.when(owner)
    def _():
        for c in dag:
            c.wait_send()

        def ag_sent(k, carry):
            ag_copy(k).wait_send()
            return carry

        lax.fori_loop(1, CHIPS, ag_sent, 0)


def shards(volume, w_early, w_deep, cotangent):
    any_ = pl.BlockSpec(memory_space=pl.ANY)
    vmem = pl.BlockSpec(memory_space=pltpu.VMEM)
    cells = volume.shape[0] * volume.shape[1] * volume.shape[2] * SPACE * FILT
    body = functools.partial(kernel, 1.0 / math.sqrt(cells), 1.0 / math.sqrt(cells // 8))
    return pl.pallas_call(
        body,
        out_shape=(
            jax.ShapeDtypeStruct((2, 64, 8, 32), BF),
            jax.ShapeDtypeStruct((27, 128, 128), F32),
            jax.ShapeDtypeStruct((27, 128, 32), F32),
        ),
        in_specs=[any_] * 4,
        out_specs=(vmem,) * 3,
        scratch_shapes=[pltpu.VMEM(*v) for v in SCRATCH.values()]
        + [pltpu.SemaphoreType.DMA(v) for v in SEMS.values()],
        compiler_params=pltpu.CompilerParams(
            collective_id=0, has_side_effects=True, vmem_limit_bytes=56 << 20
        ),
        name="step",
    )(volume, w_early.reshape(9, 384, 128), w_deep, cotangent)


def solution(mesh):
    return jax.shard_map(
        shards,
        mesh=mesh,
        in_specs=(
            P("space", "filt", None, None),
            P(),
            P(None, None, "filt"),
            P("space", None, None, "filt"),
        ),
        out_specs=(P("space", None, None, "filt"), P(), P(None, None, "filt")),
        check_vma=False,
    )
```

time: 595 us -> 80.3 us (0.13); the launches traced: 587 us -> 80 us
  waiting for transfers between devices: 318 us -> 0 us
  local copies, waits for them, and re-layouts: 87 us -> 9.8 us
  matrix products: 73.5 us -> 0 us
  Pallas kernels: 0 us -> 69.6 us
  blocking collectives: 46.6 us -> 0 us
  starting transfers between devices: 33.9 us -> 0 us
  between operations: 17.5 us -> 0.65 us
  other arithmetic: 10.6 us -> 0 us
    psum x2 -> x0, waiting for transfers between devices: 239 us -> none  [the longest x1 152 us: shards(): lax.psum(early_terms, ('space', 'filt')) / math.sqrt(early_total)]
    dot_general x135 -> x0, matrix products: 73.5 us -> none  [the longest x54 51.3 us: contract_cells(): lax.dot_general(left, right, (((0,), (0,)), ((), ())), preferred_element_...]
    pallas_call x0 -> x1, Pallas kernels: none -> 69.6 us  [shards(): pl.pallas_call(body, out_shape=(jax.ShapeDtypeStruct((2, 64, 8, 32), BF),...]
    reduce_scatter x1 -> x0, waiting for transfers between devices: 65.5 us -> none  [shards(): lax.psum_scatter(term, 'filt', scatter_dimension=3, tiled=True)]
    unnamed x194 -> x5, local copies, waits for them, and re-layouts: 59.2 us -> 5.14 us
    all_gather x1 -> x0, blocking collectives: 32.2 us -> none  [shards(): piece = lax.all_gather(slab, 'filt', axis=3, tiled=True)]
    ppermute x8 -> x0, starting transfers between devices: 29.1 us -> none  [the longest x4 18.2 us: extended(): lax.ppermute(lax.slice_in_dim(block, block.shape[dim] - width, None, axis...]
    slice x13 -> x0, local copies, waits for them, and re-layouts: 21.4 us -> none  [the longest x5 19 us: window(): source[first:first + size_x, second:second + size_y, third:third + size_z]]
  transfers between devices with their start and end apart: 12 -> 0, of which waited for: 7 -> 0; matrix products, arithmetic and copies ran while one was open for 10% -> 0% of each run, Pallas kernels for 0% -> 0%
where the time goes in v1:
time: 80.3 us; the launch traced here: 80 us
  Pallas kernels  69.6 us (87%)
  local copies, waits for them, and re-layouts  9.8 us (12%)
    pallas_call x1, Pallas kernels, shards(): pl.pallas_call(body, out_shape=(jax.ShapeDtypeStruct((2, 64, 8, 32), BF),...  69.6 us
    unnamed x5, local copies, waits for them, and re-layouts  5.14 us
    pallas_call x2, local copies, waits for them, and re-layouts, shards(): pl.pallas_call(body, out_shape=(jax.ShapeDtypeStruct((2, 64, 8, 32), BF),...  4.65 us

profile of v1, /device:TPU:1, one launch (start us, length us, event | category | flops | bytes accessed | tf_op | source)
XLA Modules:
  0.0 80.0 jit_solution(15114741163357253341)
XLA Ops:
  0.6 1.8 %copy.8.ct_in = bf16[2,64,8,32]{3,2,1,0:T(8,128)(2,1)} copy(bf16[2,64,8,32]{1,3,2,0:T(8,128)(2,1)} %param.7) | data formatting | bytes 131072 | tf_op args[3]
  2.4 2.2 %copy.7.wd_in = bf16[27,128,32]{2,1,0:T(8,128)(2,1)} copy(bf16[27,128,32]{1,2,0:T(8,128)(2,1)} %param.6) | data formatting | bytes 442368 | tf_op args[2]
  4.6 69.6 %step.1 = (bf16[2,64,8,32]{3,2,1,0:T(8,128)(2,1)}, f32[27,128,128]{2,1,0:T(8,128)}, f32[27,128,32]{2,1,0:T(8,128)}) custom-call(bf16[4,16,16,128]{3,2,1,0:T(8,128)(2,1)} %vol.1, bf16[9,384,128]{2,1,0:T(8,128)(2,1)} %bitcast.1, bf16[27,128,32]{2,1,0:T(8,128)(2,1)} %copy.7.wd_in, bf16[2,64,8,32]{3,2,1,0:T(8,128)(2,1)} %copy.8.ct_in), custom_call_target="tpu_custom_call" | custom-call | tf_op jit(solution)/shard_map/step/pallas_call | solution.py:611
  74.2 0.0 copy-start
  74.2 1.9 %copy.9 = bf16[2,64,8,32]{1,3,2,0:T(8,128)(2,1)} copy(bf16[2,64,8,32]{3,2,1,0:T(8,128)(2,1)} %get-tuple-element.3) | data formatting | bytes 131072 | tf_op jit(solution)/shard_map/step/pallas_call | solution.py:611
  76.1 2.7 %copy.10 = f32[27,128,32]{1,2,0:T(8,128)} copy(f32[27,128,32]{2,1,0:T(8,128)} %get-tuple-element.5) | data formatting | bytes 884736 | tf_op jit(solution)/shard_map/step/pallas_call | solution.py:611
  78.8 0.0 copy-done
  78.8 1.2 %copy.12 = f32[27,128,128]{2,1,0:T(8,128)} copy(f32[27,128,128]{2,1,0:T(8,128)S(1)} %copy-done) | data formatting | bytes 3538944
Async XLA Ops:
  74.2 4.7 %copy-start = (f32[27,128,128]{2,1,0:T(8,128)S(1)}, f32[27,128,128]{2,1,0:T(8,128)}, u32[]{:S(2)}) copy-start(f32[27,128,128]{2,1,0:T(8,128)} %get-tuple-element.10) | copy-start | bytes 5308420

commit v2 on v1

v2 whole, which is shorter than its diff:
```python
import functools
import math

import jax
import jax.numpy as jnp
from jax import lax
from jax.experimental import pallas as pl
from jax.experimental.pallas import tpu as pltpu
from jax.sharding import PartitionSpec as P

MESH = pl.DeviceIdType.MESH
BF = jnp.bfloat16
F32 = jnp.float32
SPACE, FILT, CHIPS = 16, 8, 64
DIRS = [(ds, df) for ds in (-1, 0, 1) for df in (-1, 0, 1) if ds or df]
GROUP = 4
DIRECT = 15
SHARE = 3
OWNERS = 7


def rcopy(src, dst, send_sem, recv_sem, device):
    return pltpu.make_async_remote_copy(
        src_ref=src,
        dst_ref=dst,
        send_sem=send_sem,
        recv_sem=recv_sem,
        device_id=device,
        device_id_type=MESH,
    )


def sigmoid(v):
    return 1.0 / (1.0 + jnp.exp(-v))


def shift_rows(v, step):
    size = v.shape[1]
    row = lax.broadcasted_iota(jnp.int32, v.shape, 1)
    edge = size - 1 if step == 1 else 0
    rolled = pltpu.roll(v, (-step) % size, 1)
    return jnp.where(row == edge, 0.0, rolled)


def dot(a, b):
    return lax.dot_general(a, b, (((1,), (0,)), ((), ())), preferred_element_type=F32)


def dot_t(a, b):
    return lax.dot_general(a, b, (((1,), (1,)), ((), ())), preferred_element_type=F32)


def edges(step, size):
    if step == 1:
        return size - 1, 0, 1
    if step == -1:
        return 0, size + 1, 1
    return 0, 1, size


def swap_cells(ref, v):
    halves = []
    for h in range(2):
        ref[h] = v[:, 128 * h : 128 * h + 128]
        rows = [ref[h, pl.ds(64 * x + n, 8, stride=8), :] for x in range(2) for n in range(8)]
        halves.append(jnp.concatenate(rows, axis=0))
    return jnp.concatenate(halves, axis=1)


class Halo:
    def __init__(self, source, base, padded, nx, ny, sems, s, f):
        self.items = []
        for k, (ds, df) in enumerate(DIRS):
            sx, dx, lx = edges(ds, nx)
            sy, dy, ly = edges(df, ny)
            src = source.at[base + sx : base + sx + lx, base + sy : base + sy + ly]
            dst = padded.at[dx : dx + lx, dy : dy + ly]
            to_s, to_f, from_s, from_f = s + ds, f + df, s - ds, f - df
            send = (to_s >= 0) & (to_s < SPACE) & (to_f >= 0) & (to_f < FILT)
            recv = (from_s >= 0) & (from_s < SPACE) & (from_f >= 0) & (from_f < FILT)
            copy = rcopy(src, dst, sems.at[0, k], sems.at[1, k], (to_s, to_f))
            self.items.append((copy, send, recv))

    def start(self):
        for copy, send, _ in self.items:
            pl.when(send)(copy.start)

    def wait_recv(self):
        for copy, _, recv in self.items:
            pl.when(recv)(copy.wait_recv)

    def wait_send(self):
        for copy, send, _ in self.items:
            pl.when(send)(copy.wait_send)


def zero_rim(padded, nx, ny, s, f):
    shape = padded.shape

    @pl.when(s == 0)
    def _():
        padded[0:1] = jnp.zeros((1,) + shape[1:], padded.dtype)

    @pl.when(s == SPACE - 1)
    def _():
        padded[nx + 1 : nx + 2] = jnp.zeros((1,) + shape[1:], padded.dtype)

    @pl.when(f == 0)
    def _():
        padded[:, 0:1] = jnp.zeros((shape[0], 1) + shape[2:], padded.dtype)

    @pl.when(f == FILT - 1)
    def _():
        padded[:, ny + 1 : ny + 2] = jnp.zeros((shape[0], 1) + shape[2:], padded.dtype)


SCRATCH = dict(
    vp=((6, 18, 16, 128), BF),
    zc=((6, 18, 16, 384), BF),
    we=((9, 384, 128), BF),
    ct=((16, 32, 64), BF),
    wg=((27, 256, 128), BF),
    cs=((8, 2, 16, 128), BF),
    cr=((2, 8, 16, 128), BF),
    acc=((1024, 128), F32),
    sg=((4, 16, 16, 128), F32),
    tmp=((16, 16, 128), F32),
    cells=((2, 128, 128), F32),
    pp=((4, 10, 8, 128), BF),
    pz=((4, 10, 8, 384), F32),
    ps=((2, 66, 8, 128), BF),
    ps3=((2, 66, 8, 384), F32),
    bs=((2, 8, 16, 128), BF),
    br=((8, 2, 16, 128), BF),
    gp=((4, 10, 8, 256), BF),
    gf=((4, 10, 8, 256), F32),
    gs=((2, 3, 8, 16, 128), BF),
    gr=((2, 3, 16, 1024), BF),
    gt=((128, 1024), BF),
    xs=((7, 64, 512), BF),
    xr=((7, 64, 512), BF),
    xo=((7, 64, 512), F32),
    es=((7, 8, 8, 512), BF),
    er=((64, 8, 512), BF),
    ea=((2, 7, 8, 8, 512), BF),
    bo=((16, 32, 64), BF),
    gd=((27, 32, 128), F32),
    pb=((1024, 1152), BF),
    hs=((48, 1152), BF),
    hr=((48, 1152), BF),
    ho=((48, 1152), F32),
    dsd=((28, 16, 128), BF),
    dr=((8, 4, 16, 128), BF),
    da=((2, 28, 16, 128), BF),
)
SEMS = dict(
    local=(4,),
    halo_v=(2, 8),
    halo_p=(2, 8),
    halo_g=(2, 8),
    s_cot=(2, 8),
    s_wa=(2, 8),
    s_wb=(2, 8),
    s_wy=(2, 4),
    s_wrel=(2, 5),
    s_ps=(2, 8),
    s_bo=(2, 8),
    s_g=(2, 8),
    s_x=(2, 7),
    s_rs=(7,),
    r_rs=(1,),
    s_ag=(1,),
    r_ag=(8,),
    s_ear=(2, 8),
    s_out=(2,),
    s_ea=(2, 8),
    s_h=(2,),
    s_drs=(2, 8),
    s_dag=(2, 8),
    s_dar=(2,),
)


def kernel(early_scale, deep_scale, vol, we_in, wd_in, ct_in, bo_out, ea_out, gd_out, *scratch):
    r = dict(zip(list(SCRATCH) + list(SEMS), scratch))
    ready = scratch[-1]
    s = lax.axis_index("space")
    f = lax.axis_index("filt")
    core = lax.rem(s, 2)
    other = 1 - core
    sib = s + 1 - 2 * core
    j = lax.div(s, 2)

    def filt_peer(k):
        return lax.rem(f + k, FILT)

    def filt_from(k):
        return lax.rem(f + FILT - k, FILT)

    chips_s = [lax.rem(s + 2 * dj, SPACE) for dj in range(8)]
    chips_f = [lax.rem(f + df, FILT) for df in range(8)]
    owner = j < OWNERS

    barrier = pltpu.get_barrier_semaphore()

    def space_chip(k):
        return lax.rem(s + 2 * k, SPACE)

    greeted = [(s, filt_peer(k)) for k in range(1, FILT)]
    greeted += [(space_chip(k), f) for k in range(1, 8)]
    greeted += [
        (lax.rem(s + d, SPACE), lax.rem(f + df, FILT))
        for d in (1, SPACE - 1)
        for df in (0, 1, FILT - 1)
    ]
    for device in greeted:
        pl.semaphore_signal(barrier, inc=1, device_id=device, device_id_type=MESH)

    own_vol = pltpu.make_async_copy(vol, r["vp"].at[1:5, 1:17], r["local"].at[0])
    own_vol.start()
    wg = r["wg"]
    w_rows = pl.ds(pl.multiple_of(128 * core + 16 * f, 16), 16)
    w_half = pl.ds(pl.multiple_of(16 * core, 16), 16)
    y = lax.div(s, 4)

    def share(yy):
        return pl.ds(DIRECT + SHARE * yy, SHARE)

    own_wd = [
        pltpu.make_async_copy(wd_in.at[taps, w_half], wg.at[taps, w_rows], r["local"].at[n])
        for n, taps in ((1, pl.ds(0, DIRECT)), (3, share(y)))
    ]
    for c in own_wd:
        c.start()
    own_ct = pltpu.make_async_copy(ct_in, r["ct"], r["local"].at[2])
    own_ct.start()
    own_ct.wait()
    lane = lax.broadcasted_iota(jnp.int32, (32, 128), 1)
    parts = [jnp.zeros((32, 128), F32)] * FILT
    for p in range(16):
        x = r["ct"][p].astype(F32)
        x = jnp.concatenate([x, x], axis=1)
        for q in range(FILT):
            moved = pltpu.roll(x, (8 * p - 8 * q) % 128, 1)
            parts[q] = jnp.where(lane // 8 == p, moved, parts[q])
    for q in range(FILT):
        r["cs"][q] = parts[q].astype(BF).reshape(2, 16, 128)
    zero_rim(r["vp"], 4, 16, s, f)
    zero_rim(r["pp"], 2, 8, s, f)
    zero_rim(r["gp"], 2, 8, s, f)
    r["ps"][:, 0:1] = jnp.zeros((2, 1, 8, 128), BF)
    r["ps"][:, 65:66] = jnp.zeros((2, 1, 8, 128), BF)

    pl.semaphore_wait(barrier, len(greeted))
    halo_v = Halo(vol, 0, r["vp"], 4, 16, r["halo_v"], s, f)
    halo_v.start()
    own_we = pltpu.make_async_copy(we_in, r["we"], r["local"].at[2])
    own_we.start()

    def w_send(taps, sems, k):
        return rcopy(
            wd_in.at[taps, w_half],
            wg.at[taps, w_rows],
            r[sems].at[0, k],
            r[sems].at[1, k],
            (s, filt_peer(k)),
        )

    for k in range(1, 8):
        pl.semaphore_signal(ready, inc=1, device_id=(space_chip(k), f), device_id_type=MESH)

    wb = []
    for k in range(1, FILT):
        wb.append(w_send(share(y), "s_wb", k))
        wb[-1].start()
    cots = []
    for k in range(1, FILT):
        cots.append(
            rcopy(
                r["cs"].at[filt_peer(k)],
                r["cr"].at[:, f],
                r["s_cot"].at[0, k],
                r["s_cot"].at[1, k],
                (s, filt_peer(k)),
            )
        )
        cots[-1].start()
    wa = []
    for k in range(1, FILT):
        wa.append(w_send(pl.ds(0, DIRECT), "s_wa", k))
        wa[-1].start()
    r["cr"][:, pl.ds(f, 1)] = r["cs"][pl.ds(f, 1)].reshape(2, 1, 16, 128)

    own_vol.wait()
    halo_v.wait_recv()
    for c in own_wd:
        c.wait()
    for c in wb:
        c.wait_recv()
    w_core = pl.ds(pl.multiple_of(128 * core, 128), 128)

    def w_pass(taps, sems, k, device):
        piece = wg.at[taps, w_core]
        return rcopy(piece, piece, r[sems].at[0, k], r[sems].at[1, k], device)

    wy = []
    for k in range(1, 4):
        wy.append(w_pass(share(y), "s_wy", k, (lax.rem(s + 4 * k, SPACE), f)))
        wy[-1].start()
    relay = [w_pass(share(y), "s_wrel", 0, (sib, f))]
    relay[-1].start()
    zc = r["zc"]
    for row in range(6):
        x = r["vp"][row].astype(F32)
        zc[row, :, :, 0:128] = shift_rows(x, -1).astype(BF)
        zc[row, :, :, 128:256] = r["vp"][row]
        zc[row, :, :, 256:384] = shift_rows(x, 1).astype(BF)
    own_we.wait()
    acc = r["acc"]
    for ab in range(9):
        a, b = ab // 3, ab % 3
        patch = zc[a : a + 4, b : b + 16].reshape(1024, 384)
        term = dot(patch, r["we"][ab])
        if ab == 0:
            acc[...] = term
        else:
            acc[...] += term
    for half in range(2):
        v = acc[512 * half : 512 * half + 512].reshape(2, 16, 16, 128)
        sig = sigmoid(v)
        r["sg"][2 * half : 2 * half + 2] = sig * (1.0 + v * (1.0 - sig)) * 0.125
        act = v * sig
        act = (act[0] + act[1]).reshape(8, 2, 16, 128)
        r["tmp"][8 * half : 8 * half + 8] = act[:, 0] + act[:, 1]
    tmp = r["tmp"]
    pooled = (tmp[:, pl.ds(0, 8, stride=2), :] + tmp[:, pl.ds(1, 8, stride=2), :]) * 0.125
    pooled = pooled.reshape(2, 8, 8, 128).astype(BF)
    r["pp"][1:3, 1:9] = pooled
    halo_p = Halo(r["pp"], 1, r["pp"], 2, 8, r["halo_p"], s, f)
    halo_p.start()
    r["ps"][:, pl.ds(1 + 8 * f, 8)] = pooled

    for c in wa:
        c.wait_recv()
    relay.append(w_pass(pl.ds(0, DIRECT), "s_wrel", 4, (sib, f)))
    relay[-1].start()
    for k in range(1, 4):
        wy[k - 1].wait_recv()
        relay.append(w_pass(share(lax.rem(y + 4 - k, 4)), "s_wrel", k, (sib, f)))
        relay[-1].start()
    for c in cots:
        c.wait_recv()
    cot = swap_cells(r["cells"], r["cr"][...].reshape(256, 128).astype(F32).T)
    halo_p.wait_recv()
    pz = r["pz"]
    for row in range(4):
        x = r["pp"][row].astype(F32)
        pz[row, :, :, 0:128] = shift_rows(x, -1)
        pz[row, :, :, 128:256] = x
        pz[row, :, :, 256:384] = shift_rows(x, 1)
    for c in relay:
        c.wait_recv()

    pre = jnp.zeros((128, 256), F32)
    for ab in range(9):
        a, b = ab // 3, ab % 3
        patch = pz[a : a + 2, b : b + 8].reshape(128, 384).astype(BF)
        taps = jnp.concatenate([wg[3 * ab + c] for c in range(3)], axis=1)
        pre = pre + dot_t(patch, taps)
    sig = sigmoid(pre)
    g = (cot * (sig * (1.0 + pre * (1.0 - sig)))).astype(BF)
    r["gp"][1:3, 1:9] = g.astype(F32).reshape(2, 8, 8, 256).astype(BF)
    halo_g = Halo(r["gp"], 1, r["gp"], 2, 8, r["halo_g"], s, f)
    halo_g.start()
    pss = []
    for k in range(1, FILT):
        pss.append(
            rcopy(
                r["pp"].at[1:3, 1:9],
                r["ps"].at[:, pl.ds(1 + 8 * f, 8)],
                r["s_ps"].at[0, k],
                r["s_ps"].at[1, k],
                (s, filt_peer(k)),
            )
        )
        pss[-1].start()
    act = swap_cells(r["cells"], pre * sig)
    r["bs"][...] = act.T.astype(BF).reshape(2, 8, 16, 128)
    bos = []
    for k in range(1, FILT):
        bos.append(
            rcopy(
                r["bs"].at[:, filt_peer(k)],
                r["br"].at[f],
                r["s_bo"].at[0, k],
                r["s_bo"].at[1, k],
                (s, filt_peer(k)),
            )
        )
        bos[-1].start()
    r["br"][pl.ds(f, 1)] = r["bs"][:, pl.ds(f, 1)].reshape(1, 2, 16, 128)

    halo_g.wait_recv()
    gf = r["gf"]
    gf[...] = r["gp"][...].astype(F32)
    back = jnp.zeros((128, 384), F32)
    for ab in range(9):
        a, b = ab // 3, ab % 3
        patch = gf[2 - a : 4 - a, 2 - b : 10 - b].reshape(128, 256).astype(BF)
        taps = jnp.concatenate([wg[3 * ab + c] for c in range(3)], axis=1)
        back = back + dot(patch, taps)
    back = back.reshape(16, 8, 384)
    gpool = (
        shift_rows(back[:, :, 0:128], 1)
        + back[:, :, 128:256]
        + shift_rows(back[:, :, 256:384], -1)
    )
    gpool = gpool.astype(BF).astype(F32)
    tmp[:, pl.ds(0, 8, stride=2), :] = gpool
    tmp[:, pl.ds(1, 8, stride=2), :] = gpool
    for row in range(4):
        spread = tmp[8 * (row // 2) : 8 * (row // 2) + 8]
        spread = jnp.broadcast_to(spread[:, None], (8, 2, 16, 128)).reshape(16, 16, 128)
        grad = (spread * r["sg"][row]).astype(BF).astype(F32).reshape(256, 128)
        r["gt"][:, 256 * row : 256 * row + 256] = grad.T.astype(BF)

    gt = r["gt"][...]
    es, er, ea = r["es"], r["er"], r["ea"]
    pl.semaphore_wait(ready, 7)

    def group_of(k):
        return lax.rem(j + k, OWNERS)

    def x_copy(k):
        return rcopy(
            r["xs"].at[k], r["xr"].at[k], r["s_x"].at[0, k], r["s_x"].at[1, k], (sib, f)
        )

    for k in range(OWNERS + 1):
        if k < OWNERS:
            patches = []
            for n in range(GROUP):
                t = jnp.minimum(GROUP * group_of(k) + n, 26)
                a, b, c = lax.div(t, 9), lax.rem(lax.div(t, 3), 3), lax.rem(t, 3)
                lanes = pl.ds(pl.multiple_of(128 * c, 128), 128)
                patch = zc[pl.ds(a, 4), pl.ds(b, 16), :, lanes]
                patches.append(patch.reshape(1024, 128))
            term = dot(gt, jnp.concatenate(patches, axis=1))

            @pl.when(core == 0)
            def _():
                r["xo"][k] = term[0:64]
                r["xs"][k] = term[64:128].astype(BF)

            @pl.when(core == 1)
            def _():
                r["xo"][k] = term[64:128]
                r["xs"][k] = term[0:64].astype(BF)

            x_copy(k).start()
        if k >= 1:
            p = k - 1
            x_copy(p).wait_recv()
            total = r["xo"][p] + r["xr"][p].astype(F32)
            es[p] = total.reshape(8, 8, 512).astype(BF)
            to_j = group_of(p)
            dj = lax.rem(to_j - j + 8, 8)
            for df in range(8):
                copy = rcopy(
                    es.at[p, chips_f[df]],
                    er.at[8 * dj + df],
                    r["s_rs"].at[p],
                    r["r_rs"].at[0],
                    (2 * to_j + core, chips_f[df]),
                )
                if p == 0 and df == 0:
                    pl.when(j >= OWNERS)(copy.start)
                else:
                    copy.start()

    for a in range(3):
        piece = gf[2 - a : 4 - a, 1:9].reshape(128, 256)
        r["gs"][:, a] = piece.T.astype(BF).reshape(2, 8, 16, 128)
    gcs = []
    lanes = pl.ds(pl.multiple_of(128 * f, 128), 128)
    for k in range(1, FILT):
        gcs.append(
            rcopy(
                r["gs"].at[:, :, filt_peer(k)],
                r["gr"].at[:, :, :, lanes],
                r["s_g"].at[0, k],
                r["s_g"].at[1, k],
                (s, filt_peer(k)),
            )
        )
        gcs[-1].start()
    r["gr"][:, :, :, lanes] = r["gs"][:, :, pl.ds(f, 1)].reshape(2, 3, 16, 128)

    for c in pss:
        c.wait_recv()
    ps3 = r["ps3"]
    for row in range(2):
        x = r["ps"][row].astype(F32)
        ps3[row, :, :, 0:128] = shift_rows(x, -1)
        ps3[row, :, :, 128:256] = x
        ps3[row, :, :, 256:384] = shift_rows(x, 1)
    for q in range(8):
        for b in range(3):
            patch = ps3[:, 8 * q + b : 8 * q + b + 8].reshape(128, 384).astype(BF)
            r["pb"][128 * q : 128 * q + 128, 384 * b : 384 * b + 384] = patch
    for c in gcs:
        c.wait_recv()
    deep = dot(r["gr"][...].reshape(96, 1024), r["pb"][...])

    @pl.when(core == 0)
    def _():
        r["ho"][...] = deep[0:48]
        r["hs"][...] = deep[48:96].astype(BF)

    @pl.when(core == 1)
    def _():
        r["ho"][...] = deep[48:96]
        r["hs"][...] = deep[0:48].astype(BF)

    hcopy = rcopy(r["hs"], r["hr"], r["s_h"].at[0], r["s_h"].at[1], (sib, f))
    hcopy.start()

    for c in bos:
        c.wait_recv()
    parts = [jnp.zeros((32, 128), F32)] * 16
    for q in range(FILT):
        x = r["br"][q].reshape(32, 128).astype(F32)
        for p in range(16):
            moved = pltpu.roll(x, (8 * q - 8 * p) % 128, 1)
            parts[p] = jnp.where(lane // 8 == q, moved, parts[p])
    for p in range(16):
        r["bo"][p] = parts[p][:, 0:64].astype(BF)
    bo_copy = pltpu.make_async_copy(r["bo"], bo_out, r["s_out"].at[0])
    bo_copy.start()

    hcopy.wait_recv()
    dsd = r["dsd"]
    dsd[27:28] = jnp.zeros((1, 16, 128), BF)
    total = r["ho"][...] + r["hr"][...].astype(F32)
    for a in range(3):
        for bc in range(9):
            dsd[9 * a + bc] = total[16 * a : 16 * a + 16, 128 * bc : 128 * bc + 128].astype(BF)

    def first_of(jj):
        return jnp.minimum(GROUP * jj, GROUP * (OWNERS - 1))

    drs = []
    for k in range(1, 8):
        to_s = space_chip(k)
        to_j = lax.div(to_s, 2)
        copy = rcopy(
            dsd.at[pl.ds(first_of(to_j), GROUP)],
            r["dr"].at[k],
            r["s_drs"].at[0, k],
            r["s_drs"].at[1, k],
            (to_s, f),
        )
        pl.when(to_j < OWNERS)(copy.start)
        drs.append((copy, to_j < OWNERS))

    mine_t = pl.ds(first_of(j), GROUP)

    ag_sends = []
    for k in range(1, CHIPS):
        piece = ea.at[core, jnp.minimum(j, OWNERS - 1), f]
        device = (chips_s[k // 8], chips_f[k % 8])
        ag_sends.append(rcopy(piece, piece, r["s_ag"].at[0], r["r_ag"].at[k // 8], device))

    @pl.when(owner)
    def _():
        er[0] = es[0, pl.ds(f, 1)].reshape(8, 512)
        landed = er.at[1:CHIPS]
        rcopy(landed, landed, r["s_rs"].at[0], r["r_rs"].at[0], (s, f)).wait_recv()
        total = jnp.sum(er[0:8].astype(F32), axis=0)
        for n in range(1, 8):
            total = total + jnp.sum(er[8 * n : 8 * n + 8].astype(F32), axis=0)
        total = (total * early_scale).astype(BF).reshape(1, 1, 1, 8, 512)
        ea[pl.ds(core, 1), pl.ds(j, 1), pl.ds(f, 1)] = total
        for c in ag_sends:
            c.start()

    da = r["da"]
    piece = da.at[core, mine_t]
    dag = []
    for k in range(1, 8):
        dag.append(
            rcopy(piece, piece, r["s_dag"].at[0, k], r["s_dag"].at[1, k], (space_chip(k), f))
        )

    @pl.when(owner)
    def _():
        total = dsd[mine_t].astype(F32)
        for k in range(1, 8):
            drs[k - 1][0].wait_recv()
            total = total + r["dr"][k].astype(F32)
        da[pl.ds(core, 1), mine_t] = (total * deep_scale).astype(BF).reshape(1, GROUP, 16, 128)
        for c in dag:
            c.start()

    for k in range(1, 8):
        from_j = lax.div(lax.rem(s + SPACE - 2 * k, SPACE), 2)
        pl.when(from_j < OWNERS)(dag[k - 1].wait_recv)
    dar = rcopy(da.at[core], da.at[core], r["s_dar"].at[0], r["s_dar"].at[1], (sib, f))
    dar.start()

    dar.wait_recv()
    for t in range(27):
        r["gd"][t] = da[:, t].reshape(32, 128).astype(F32)
    gd_copy = pltpu.make_async_copy(r["gd"], gd_out, r["s_out"].at[1])
    gd_copy.start()

    def ear_copy(dj):
        piece = ea.at[core, lax.rem(j - dj + 8, 8)]
        return rcopy(piece, piece, r["s_ear"].at[0, dj], r["s_ear"].at[1, dj], (sib, f))

    def ea_copy(half, dj):
        g = lax.rem(j - dj + 8, 8)
        return pltpu.make_async_copy(ea.at[half, g], ea_out.at[half, g], r["s_ea"].at[half, dj])

    for dj in range(8):

        @pl.when(lax.rem(j - dj + 8, 8) < OWNERS)
        def _():
            landed = ea.at[core, lax.rem(j - dj + 8, 8), 0 : (8 if dj else 7)]
            rcopy(landed, landed, r["s_ag"].at[0], r["r_ag"].at[dj], (s, f)).wait_recv()
            ear_copy(dj).start()
            ea_copy(core, dj).start()

    for dj in range(8):

        @pl.when(lax.rem(j - dj + 8, 8) < OWNERS)
        def _():
            ear_copy(dj).wait_recv()
            ea_copy(other, dj).start()

    for h in (halo_v, halo_p, halo_g):
        h.wait_send()
    for c in cots + wa + wb + wy + relay + pss + bos + gcs + [hcopy, dar]:
        c.wait_send()
    for copy, active in drs:
        pl.when(active)(copy.wait_send)

    for k in range(OWNERS):
        x_copy(k).wait_send()

    def rs_sent(k, count):
        left = es.at[k, 0:count]
        rcopy(left, left, r["s_rs"].at[k], r["r_rs"].at[0], (s, f)).wait_send()

    for k in range(1, OWNERS):
        rs_sent(k, 8)

    @pl.when(owner)
    def _():
        rs_sent(0, 7)
        left = er.at[1:CHIPS]
        rcopy(left, left, r["s_ag"].at[0], r["r_rs"].at[0], (s, f)).wait_send()
        for c in dag:
            c.wait_send()

    pl.when(j >= OWNERS)(functools.partial(rs_sent, 0, 8))
    for dj in range(8):

        @pl.when(lax.rem(j - dj + 8, 8) < OWNERS)
        def _():
            ear_copy(dj).wait_send()
            ea_copy(core, dj).wait()
            ea_copy(other, dj).wait()

    bo_copy.wait()
    gd_copy.wait()


def results(bo_in, ea_in, gd_in, bo_out, ge_out, gd_out, bo, ea, gd, ge, sems):
    ins = [pltpu.make_async_copy(ea_in.at[:, g], ea.at[g], sems.at[0, g]) for g in range(OWNERS)]
    ins.append(pltpu.make_async_copy(bo_in, bo, sems.at[0, 7]))
    ins.append(pltpu.make_async_copy(gd_in, gd, sems.at[0, 8]))
    outs = []
    for g in range(OWNERS):
        taps = min(GROUP, 27 - GROUP * g)
        src, dst = ge.at[pl.ds(GROUP * g, taps)], ge_out.at[pl.ds(GROUP * g, taps)]
        outs.append(pltpu.make_async_copy(src, dst, sems.at[1, g]))
    outs.append(pltpu.make_async_copy(bo, bo_out, sems.at[1, 7]))
    outs.append(pltpu.make_async_copy(gd, gd_out, sems.at[1, 8]))
    for c in ins:
        c.start()
    for g in range(OWNERS):
        ins[g].wait()
        block = ea[g].reshape(128, 512).astype(F32)
        for t in range(GROUP * g, min(GROUP * g + GROUP, 27)):
            n = t - GROUP * g
            ge[t] = block[:, 128 * n : 128 * n + 128].T
        outs[g].start()
    for n in (7, 8):
        ins[n].wait()
        outs[n].start()
    for c in outs:
        c.wait()


def shards(volume, w_early, w_deep, cotangent):
    any_ = pl.BlockSpec(memory_space=pl.ANY)
    cells = volume.shape[0] * volume.shape[1] * volume.shape[2] * SPACE * FILT
    body = functools.partial(kernel, 1.0 / math.sqrt(cells), 1.0 / math.sqrt(cells // 8))
    block, early, deep = pl.pallas_call(
        body,
        out_shape=(
            jax.ShapeDtypeStruct((16, 32, 64), BF),
            jax.ShapeDtypeStruct((2, 7, 8, 8, 512), BF),
            jax.ShapeDtypeStruct((27, 32, 128), F32),
        ),
        in_specs=[any_] * 4,
        out_specs=(any_,) * 3,
        scratch_shapes=[pltpu.VMEM(*v) for v in SCRATCH.values()]
        + [pltpu.SemaphoreType.DMA(v) for v in SEMS.values()]
        + [pltpu.SemaphoreType.REGULAR],
        compiler_params=pltpu.CompilerParams(
            collective_id=0, has_side_effects=True, vmem_limit_bytes=56 << 20
        ),
        name="step",
    )(
        volume,
        w_early.reshape(9, 384, 128),
        w_deep.transpose(0, 2, 1),
        cotangent.transpose(0, 2, 3, 1).reshape(16, 32, 64),
    )
    block, early, deep = pl.pallas_call(
        results,
        out_shape=(
            jax.ShapeDtypeStruct((16, 32, 64), BF),
            jax.ShapeDtypeStruct((27, 128, 128), F32),
            jax.ShapeDtypeStruct((27, 32, 128), F32),
        ),
        in_specs=[any_] * 3,
        out_specs=(any_,) * 3,
        scratch_shapes=[
            pltpu.VMEM((16, 32, 64), BF),
            pltpu.VMEM((7, 2, 8, 8, 512), BF),
            pltpu.VMEM((27, 32, 128), F32),
            pltpu.VMEM((27, 128, 128), F32),
            pltpu.SemaphoreType.DMA((2, 9)),
        ],
        compiler_params=pltpu.CompilerParams(vmem_limit_bytes=60 << 20),
        name="results",
    )(block, early, deep)
    block = block.reshape(2, 8, 32, 64).transpose(0, 3, 1, 2)
    return block, early, deep.transpose(0, 2, 1)


def solution(mesh):
    return jax.shard_map(
        shards,
        mesh=mesh,
        in_specs=(
            P("space", "filt", None, None),
            P(),
            P(None, None, "filt"),
            P("space", None, None, "filt"),
        ),
        out_specs=(P("space", None, None, "filt"), P(), P(None, None, "filt")),
        check_vma=False,
    )
```

time: 80.3 us -> 65.3 us (0.81)
  local copies, waits for them, and re-layouts: 9.8 us -> 0 us
  Pallas kernels: 69.6 us -> 64.5 us
    unnamed x5 -> x0, local copies, waits for them, and re-layouts: 5.14 us -> none
    pallas_call x1 -> x2, Pallas kernels: 69.6 us -> 64.5 us  [the longest x1 61.9 us: shards(): pl.pallas_call(body, out_shape=(jax.ShapeDtypeStruct((16, 32, 64), BF), j...]
    pallas_call x2 -> x0, local copies, waits for them, and re-layouts: 4.65 us -> none  [shards(): pl.pallas_call(body, out_shape=(jax.ShapeDtypeStruct((2, 64, 8, 32), BF),...]
where the time goes in v2:
time: 65.3 us; the launch traced here: 65.2 us
  Pallas kernels  64.5 us (99%)
    pallas_call x1, Pallas kernels, shards(): pl.pallas_call(body, out_shape=(jax.ShapeDtypeStruct((16, 32, 64), BF), j...  61.9 us
    pallas_call x1, Pallas kernels, shards(): pl.pallas_call(results, out_shape=(jax.ShapeDtypeStruct((16, 32, 64), BF)...  2.67 us

profile of v2, /device:TPU:1, one launch (start us, length us, event | category | flops | bytes accessed | tf_op | source)
XLA Modules:
  0.0 65.2 jit_solution(8227590740712830418)
XLA Ops:
  0.6 61.9 %step.1 = (bf16[16,32,64]{2,1,0:T(8,128)(2,1)}, bf16[2,7,8,8,512]{4,3,2,1,0:T(8,128)(2,1)}, f32[27,32,128]{2,1,0:T(8,128)}) custom-call(bf16[4,16,16,128]{3,2,1,0:T(8,128)(2,1)} %vol.1, bf16[9,384,128]{2,1,0:T(8,128)(2,1)} %bitcast.9, bf16[27,32,128]{2,1,0:T(8,128)(2,1)} %bitcast.10, bf16[16,32,64]{2,1,0:T(8,128)(2,1)} %bitcast.11), custom_call_target="tpu_custom_call" | custom-call | tf_op jit(solution)/shard_map/step/pallas_call | solution.py:710
  62.5 2.7 %results.1 = (bf16[16,32,64]{2,1,0:T(8,128)(2,1)}, f32[27,128,128]{2,1,0:T(8,128)}, f32[27,32,128]{2,1,0:T(8,128)}) custom-call(bf16[16,32,64]{2,1,0:T(8,128)(2,1)} %get-tuple-element.9.bo_in, bf16[2,7,8,8,512]{4,3,2,1,0:T(8,128)(2,1)} %get-tuple-element.10.ea_in, f32[27,32,128]{2,1,0:T(8,128)} %get-tuple-element.11.gd_in), custom_call_target="tpu_custom_call" | custom-call | tf_op jit(solution)/shard_map/results/pallas_call | solution.py:732

commit v3 on v2

--- a/solution.py
+++ b/solution.py
@@ -50,12 +50,12 @@
     return lax.dot_general(a, b, (((1,), (1,)), ((), ())), preferred_element_type=F32)
 
 
-def edges(step, size):
+def edges(step, size, width):
     if step == 1:
-        return size - 1, 0, 1
+        return size - width, 0, width
     if step == -1:
-        return 0, size + 1, 1
-    return 0, 1, size
+        return 0, size + width, width
+    return 0, width, size
 
 
 def swap_cells(ref, v):
@@ -68,11 +68,11 @@
 
 
 class Halo:
-    def __init__(self, source, base, padded, nx, ny, sems, s, f):
+    def __init__(self, source, base, padded, nx, ny, width, sems, s, f):
         self.items = []
         for k, (ds, df) in enumerate(DIRS):
-            sx, dx, lx = edges(ds, nx)
-            sy, dy, ly = edges(df, ny)
+            sx, dx, lx = edges(ds, nx, width)
+            sy, dy, ly = edges(df, ny, width)
             src = source.at[base + sx : base + sx + lx, base + sy : base + sy + ly]
             dst = padded.at[dx : dx + lx, dy : dy + ly]
             to_s, to_f, from_s, from_f = s + ds, f + df, s - ds, f - df
@@ -94,24 +94,25 @@
             pl.when(send)(copy.wait_send)
 
 
-def zero_rim(padded, nx, ny, s, f):
+def zero_rim(padded, nx, ny, width, s, f):
     shape = padded.shape
+    w = width
 
     @pl.when(s == 0)
     def _():
-        padded[0:1] = jnp.zeros((1,) + shape[1:], padded.dtype)
+        padded[0:w] = jnp.zeros((w,) + shape[1:], padded.dtype)
 
     @pl.when(s == SPACE - 1)
     def _():
-        padded[nx + 1 : nx + 2] = jnp.zeros((1,) + shape[1:], padded.dtype)
+        padded[nx + w : nx + 2 * w] = jnp.zeros((w,) + shape[1:], padded.dtype)
 
     @pl.when(f == 0)
     def _():
-        padded[:, 0:1] = jnp.zeros((shape[0], 1) + shape[2:], padded.dtype)
+        padded[:, 0:w] = jnp.zeros((shape[0], w) + shape[2:], padded.dtype)
 
     @pl.when(f == FILT - 1)
     def _():
-        padded[:, ny + 1 : ny + 2] = jnp.zeros((shape[0], 1) + shape[2:], padded.dtype)
+        padded[:, ny + w : ny + 2 * w] = jnp.zeros((shape[0], w) + shape[2:], padded.dtype)
 
 
 SCRATCH = dict(
@@ -120,19 +121,19 @@
     we=((9, 384, 128), BF),
     ct=((16, 32, 64), BF),
     wg=((27, 256, 128), BF),
-    cs=((8, 2, 16, 128), BF),
-    cr=((2, 8, 16, 128), BF),
+    cs=((8, 2, 2, 16, 128), BF),
+    cr=((4, 2, 8, 16, 128), BF),
     acc=((1024, 128), F32),
     sg=((4, 16, 16, 128), F32),
     tmp=((16, 16, 128), F32),
     cells=((2, 128, 128), F32),
-    pp=((4, 10, 8, 128), BF),
-    pz=((4, 10, 8, 384), F32),
+    act=((128, 256), F32),
+    pp=((6, 12, 8, 128), BF),
+    pz=((6, 12, 8, 384), F32),
     ps=((2, 66, 8, 128), BF),
     ps3=((2, 66, 8, 384), F32),
     bs=((2, 8, 16, 128), BF),
     br=((8, 2, 16, 128), BF),
-    gp=((4, 10, 8, 256), BF),
     gf=((4, 10, 8, 256), F32),
     gs=((2, 3, 8, 16, 128), BF),
     gr=((2, 3, 16, 1024), BF),
@@ -157,8 +158,7 @@
     local=(4,),
     halo_v=(2, 8),
     halo_p=(2, 8),
-    halo_g=(2, 8),
-    s_cot=(2, 8),
+    s_cot=(2, 3),
     s_wa=(2, 8),
     s_wb=(2, 8),
     s_wy=(2, 4),
@@ -211,7 +211,7 @@
     greeted += [
         (lax.rem(s + d, SPACE), lax.rem(f + df, FILT))
         for d in (1, SPACE - 1)
-        for df in (0, 1, FILT - 1)
+        for df in range(FILT)
     ]
     for device in greeted:
         pl.semaphore_signal(barrier, inc=1, device_id=device, device_id_type=MESH)
@@ -236,23 +236,33 @@
     own_ct.start()
     own_ct.wait()
     lane = lax.broadcasted_iota(jnp.int32, (32, 128), 1)
-    parts = [jnp.zeros((32, 128), F32)] * FILT
-    for p in range(16):
-        x = r["ct"][p].astype(F32)
-        x = jnp.concatenate([x, x], axis=1)
+    for x in range(2):
+        parts = [jnp.zeros((32, 128), F32)] * FILT
+        for z in range(8):
+            v = r["ct"][8 * x + z].astype(F32)
+            v = jnp.concatenate([v, jnp.zeros_like(v)], axis=1)
+            here = (lane >= 16 * z) & (lane < 16 * z + 10)
+            for q in range(FILT):
+                moved = pltpu.roll(v, (16 * z - 8 * q + 1) % 128, 1)
+                parts[q] = jnp.where(here, moved, parts[q])
         for q in range(FILT):
-            moved = pltpu.roll(x, (8 * p - 8 * q) % 128, 1)
-            parts[q] = jnp.where(lane // 8 == p, moved, parts[q])
-    for q in range(FILT):
-        r["cs"][q] = parts[q].astype(BF).reshape(2, 16, 128)
-    zero_rim(r["vp"], 4, 16, s, f)
-    zero_rim(r["pp"], 2, 8, s, f)
-    zero_rim(r["gp"], 2, 8, s, f)
+            r["cs"][q, x] = parts[q].astype(BF).reshape(2, 16, 128)
+
+    @pl.when(s == 0)
+    def _():
+        r["cr"][0] = jnp.zeros((2, 8, 16, 128), BF)
+
+    @pl.when(s == SPACE - 1)
+    def _():
+        r["cr"][3] = jnp.zeros((2, 8, 16, 128), BF)
+
+    zero_rim(r["vp"], 4, 16, 1, s, f)
+    zero_rim(r["pp"], 2, 8, 2, s, f)
     r["ps"][:, 0:1] = jnp.zeros((2, 1, 8, 128), BF)
     r["ps"][:, 65:66] = jnp.zeros((2, 1, 8, 128), BF)
 
     pl.semaphore_wait(barrier, len(greeted))
-    halo_v = Halo(vol, 0, r["vp"], 4, 16, r["halo_v"], s, f)
+    halo_v = Halo(vol, 0, r["vp"], 4, 16, 1, r["halo_v"], s, f)
     halo_v.start()
     own_we = pltpu.make_async_copy(we_in, r["we"], r["local"].at[2])
     own_we.start()
@@ -273,23 +283,35 @@
     for k in range(1, FILT):
         wb.append(w_send(share(y), "s_wb", k))
         wb[-1].start()
-    cots = []
-    for k in range(1, FILT):
-        cots.append(
-            rcopy(
-                r["cs"].at[filt_peer(k)],
-                r["cr"].at[:, f],
-                r["s_cot"].at[0, k],
-                r["s_cot"].at[1, k],
-                (s, filt_peer(k)),
-            )
-        )
-        cots[-1].start()
+
     wa = []
     for k in range(1, FILT):
         wa.append(w_send(pl.ds(0, DIRECT), "s_wa", k))
         wa[-1].start()
-    r["cr"][:, pl.ds(f, 1)] = r["cs"][pl.ds(f, 1)].reshape(2, 1, 16, 128)
+
+    def cot_copy(src, row, n, device):
+        return rcopy(
+            src, r["cr"].at[row, :, f], r["s_cot"].at[0, n], r["s_cot"].at[1, n], device
+        )
+
+    def cot_all(n):
+        whole = r["cs"].at[0:7] if n == 0 else r["cr"].at[0]
+        return rcopy(whole, whole, r["s_cot"].at[0, n], r["s_cot"].at[1, n], (s, f))
+
+    for k in range(1, FILT):
+        cot_copy(r["cs"].at[filt_peer(k)], slice(1, 3), 0, (s, filt_peer(k))).start()
+
+    @pl.when(s > 0)
+    def _():
+        for q in range(FILT):
+            cot_copy(r["cs"].at[q, 0], 3, 1, (s - 1, q)).start()
+
+    @pl.when(s < SPACE - 1)
+    def _():
+        for q in range(FILT):
+            cot_copy(r["cs"].at[q, 1], 0, 2, (s + 1, q)).start()
+
+    r["cr"][1:3, :, pl.ds(f, 1)] = r["cs"][pl.ds(f, 1)].reshape(2, 2, 1, 16, 128)
 
     own_vol.wait()
     halo_v.wait_recv()
@@ -335,8 +357,8 @@
     tmp = r["tmp"]
     pooled = (tmp[:, pl.ds(0, 8, stride=2), :] + tmp[:, pl.ds(1, 8, stride=2), :]) * 0.125
     pooled = pooled.reshape(2, 8, 8, 128).astype(BF)
-    r["pp"][1:3, 1:9] = pooled
-    halo_p = Halo(r["pp"], 1, r["pp"], 2, 8, r["halo_p"], s, f)
+    r["pp"][2:4, 2:10] = pooled
+    halo_p = Halo(r["pp"], 2, r["pp"], 2, 8, 2, r["halo_p"], s, f)
     halo_p.start()
     r["ps"][:, pl.ds(1 + 8 * f, 8)] = pooled
 
@@ -348,12 +370,23 @@
         wy[k - 1].wait_recv()
         relay.append(w_pass(share(lax.rem(y + 4 - k, 4)), "s_wrel", k, (sib, f)))
         relay[-1].start()
-    for c in cots:
-        c.wait_recv()
-    cot = swap_cells(r["cells"], r["cr"][...].reshape(256, 128).astype(F32).T)
+    cot_all(0).wait_recv()
+    pl.when(s > 0)(cot_all(2).wait_recv)
+    pl.when(s < SPACE - 1)(cot_all(1).wait_recv)
+    cells = r["cells"]
+    cot = []
+    for row in range(4):
+        v = r["cr"][row].reshape(256, 128).astype(F32).T
+        halves = []
+        for h in range(2):
+            cells[h] = v[:, 128 * h : 128 * h + 128]
+            cols = [cells[h, pl.ds(col, 8, stride=16), :] for col in range(10)]
+            halves.append(jnp.concatenate(cols, axis=0))
+        cot.append(jnp.concatenate(halves, axis=1))
+    cot = jnp.concatenate(cot, axis=0)
     halo_p.wait_recv()
     pz = r["pz"]
-    for row in range(4):
+    for row in range(6):
         x = r["pp"][row].astype(F32)
         pz[row, :, :, 0:128] = shift_rows(x, -1)
         pz[row, :, :, 128:256] = x
@@ -361,22 +394,11 @@
     for c in relay:
         c.wait_recv()
 
-    pre = jnp.zeros((128, 256), F32)
-    for ab in range(9):
-        a, b = ab // 3, ab % 3
-        patch = pz[a : a + 2, b : b + 8].reshape(128, 384).astype(BF)
-        taps = jnp.concatenate([wg[3 * ab + c] for c in range(3)], axis=1)
-        pre = pre + dot_t(patch, taps)
-    sig = sigmoid(pre)
-    g = (cot * (sig * (1.0 + pre * (1.0 - sig)))).astype(BF)
-    r["gp"][1:3, 1:9] = g.astype(F32).reshape(2, 8, 8, 256).astype(BF)
-    halo_g = Halo(r["gp"], 1, r["gp"], 2, 8, r["halo_g"], s, f)
-    halo_g.start()
     pss = []
     for k in range(1, FILT):
         pss.append(
             rcopy(
-                r["pp"].at[1:3, 1:9],
+                r["pp"].at[2:4, 2:10],
                 r["ps"].at[:, pl.ds(1 + 8 * f, 8)],
                 r["s_ps"].at[0, k],
                 r["s_ps"].at[1, k],
@@ -384,25 +406,18 @@
             )
         )
         pss[-1].start()
-    act = swap_cells(r["cells"], pre * sig)
-    r["bs"][...] = act.T.astype(BF).reshape(2, 8, 16, 128)
-    bos = []
-    for k in range(1, FILT):
-        bos.append(
-            rcopy(
-                r["bs"].at[:, filt_peer(k)],
-                r["br"].at[f],
-                r["s_bo"].at[0, k],
-                r["s_bo"].at[1, k],
-                (s, filt_peer(k)),
-            )
-        )
-        bos[-1].start()
-    r["br"][pl.ds(f, 1)] = r["bs"][:, pl.ds(f, 1)].reshape(1, 2, 16, 128)
-
-    halo_g.wait_recv()
+
+    pre = jnp.zeros((320, 256), F32)
+    for ab in range(9):
+        a, b = ab // 3, ab % 3
+        patch = pz[a : a + 4, b : b + 10].reshape(320, 384).astype(BF)
+        taps = jnp.concatenate([wg[3 * ab + c] for c in range(3)], axis=1)
+        pre = pre + dot_t(patch, taps)
+    sig = sigmoid(pre)
+    g = (cot * (sig * (1.0 + pre * (1.0 - sig)))).astype(BF)
     gf = r["gf"]
-    gf[...] = r["gp"][...].astype(F32)
+    gf[...] = g.astype(F32).reshape(4, 10, 8, 256)
+    r["act"][...] = (pre * sig).reshape(4, 10, 8, 256)[1:3, 1:9].reshape(128, 256)
     back = jnp.zeros((128, 384), F32)
     for ab in range(9):
         a, b = ab // 3, ab % 3
@@ -436,6 +451,26 @@
             r["xs"].at[k], r["xr"].at[k], r["s_x"].at[0, k], r["s_x"].at[1, k], (sib, f)
         )
 
+    gcs = []
+    lanes_f = pl.ds(pl.multiple_of(128 * f, 128), 128)
+
+    def send_gradients():
+        for a in range(3):
+            piece = gf[2 - a : 4 - a, 1:9].reshape(128, 256)
+            r["gs"][:, a] = piece.T.astype(BF).reshape(2, 8, 16, 128)
+        for k in range(1, FILT):
+            gcs.append(
+                rcopy(
+                    r["gs"].at[:, :, filt_peer(k)],
+                    r["gr"].at[:, :, :, lanes_f],
+                    r["s_g"].at[0, k],
+                    r["s_g"].at[1, k],
+                    (s, filt_peer(k)),
+                )
+            )
+            gcs[-1].start()
+        r["gr"][:, :, :, lanes_f] = r["gs"][:, :, pl.ds(f, 1)].reshape(2, 3, 16, 128)
+
     for k in range(OWNERS + 1):
         if k < OWNERS:
             patches = []
@@ -458,6 +493,8 @@
                 r["xs"][k] = term[0:64].astype(BF)
 
             x_copy(k).start()
+        if k == 1:
+            send_gradients()
         if k >= 1:
             p = k - 1
             x_copy(p).wait_recv()
@@ -478,24 +515,6 @@
                 else:
                     copy.start()
 
-    for a in range(3):
-        piece = gf[2 - a : 4 - a, 1:9].reshape(128, 256)
-        r["gs"][:, a] = piece.T.astype(BF).reshape(2, 8, 16, 128)
-    gcs = []
-    lanes = pl.ds(pl.multiple_of(128 * f, 128), 128)
-    for k in range(1, FILT):
-        gcs.append(
-            rcopy(
-                r["gs"].at[:, :, filt_peer(k)],
-                r["gr"].at[:, :, :, lanes],
-                r["s_g"].at[0, k],
-                r["s_g"].at[1, k],
-                (s, filt_peer(k)),
-            )
-        )
-        gcs[-1].start()
-    r["gr"][:, :, :, lanes] = r["gs"][:, :, pl.ds(f, 1)].reshape(2, 3, 16, 128)
-
     for c in pss:
         c.wait_recv()
     ps3 = r["ps3"]
@@ -525,18 +544,41 @@
     hcopy = rcopy(r["hs"], r["hr"], r["s_h"].at[0], r["s_h"].at[1], (sib, f))
     hcopy.start()
 
-    for c in bos:
-        c.wait_recv()
-    parts = [jnp.zeros((32, 128), F32)] * 16
-    for q in range(FILT):
-        x = r["br"][q].reshape(32, 128).astype(F32)
-        for p in range(16):
-            moved = pltpu.roll(x, (8 * q - 8 * p) % 128, 1)
-            parts[p] = jnp.where(lane // 8 == q, moved, parts[p])
-    for p in range(16):
-        r["bo"][p] = parts[p][:, 0:64].astype(BF)
-    bo_copy = pltpu.make_async_copy(r["bo"], bo_out, r["s_out"].at[0])
-    bo_copy.start()
+
+    act = swap_cells(r["cells"], r["act"][...])
+    r["bs"][...] = act.T.astype(BF).reshape(2, 8, 16, 128)
+    bos = []
+    for k in range(1, FILT):
+        bos.append(
+            rcopy(
+                r["bs"].at[:, filt_peer(k)],
+                r["br"].at[f],
+                r["s_bo"].at[0, k],
+                r["s_bo"].at[1, k],
+                (s, filt_peer(k)),
+            )
+        )
+        bos[-1].start()
+    r["br"][pl.ds(f, 1)] = r["bs"][:, pl.ds(f, 1)].reshape(1, 2, 16, 128)
+
+    ag_sends = []
+    for k in range(1, CHIPS):
+        piece = ea.at[core, jnp.minimum(j, OWNERS - 1), f]
+        device = (chips_s[k // 8], chips_f[k % 8])
+        ag_sends.append(rcopy(piece, piece, r["s_ag"].at[0], r["r_ag"].at[k // 8], device))
+
+    @pl.when(owner)
+    def _():
+        er[0] = es[0, pl.ds(f, 1)].reshape(8, 512)
+        landed = er.at[1:CHIPS]
+        rcopy(landed, landed, r["s_rs"].at[0], r["r_rs"].at[0], (s, f)).wait_recv()
+        total = jnp.sum(er[0:8].astype(F32), axis=0)
+        for n in range(1, 8):
+            total = total + jnp.sum(er[8 * n : 8 * n + 8].astype(F32), axis=0)
+        total = (total * early_scale).astype(BF).reshape(1, 1, 1, 8, 512)
+        ea[pl.ds(core, 1), pl.ds(j, 1), pl.ds(f, 1)] = total
+        for c in ag_sends:
+            c.start()
 
     hcopy.wait_recv()
     dsd = r["dsd"]
@@ -565,24 +607,18 @@
 
     mine_t = pl.ds(first_of(j), GROUP)
 
-    ag_sends = []
-    for k in range(1, CHIPS):
-        piece = ea.at[core, jnp.minimum(j, OWNERS - 1), f]
-        device = (chips_s[k // 8], chips_f[k % 8])
-        ag_sends.append(rcopy(piece, piece, r["s_ag"].at[0], r["r_ag"].at[k // 8], device))
-
-    @pl.when(owner)
-    def _():
-        er[0] = es[0, pl.ds(f, 1)].reshape(8, 512)
-        landed = er.at[1:CHIPS]
-        rcopy(landed, landed, r["s_rs"].at[0], r["r_rs"].at[0], (s, f)).wait_recv()
-        total = jnp.sum(er[0:8].astype(F32), axis=0)
-        for n in range(1, 8):
-            total = total + jnp.sum(er[8 * n : 8 * n + 8].astype(F32), axis=0)
-        total = (total * early_scale).astype(BF).reshape(1, 1, 1, 8, 512)
-        ea[pl.ds(core, 1), pl.ds(j, 1), pl.ds(f, 1)] = total
-        for c in ag_sends:
-            c.start()
+    for c in bos:
+        c.wait_recv()
+    parts = [jnp.zeros((32, 128), F32)] * 16
+    for q in range(FILT):
+        x = r["br"][q].reshape(32, 128).astype(F32)
+        for p in range(16):
+            moved = pltpu.roll(x, (8 * q - 8 * p) % 128, 1)
+            parts[p] = jnp.where(lane // 8 == q, moved, parts[p])
+    for p in range(16):
+        r["bo"][p] = parts[p][:, 0:64].astype(BF)
+    bo_copy = pltpu.make_async_copy(r["bo"], bo_out, r["s_out"].at[0])
+    bo_copy.start()
 
     da = r["da"]
     piece = da.at[core, mine_t]
@@ -602,18 +638,6 @@
         for c in dag:
             c.start()
 
-    for k in range(1, 8):
-        from_j = lax.div(lax.rem(s + SPACE - 2 * k, SPACE), 2)
-        pl.when(from_j < OWNERS)(dag[k - 1].wait_recv)
-    dar = rcopy(da.at[core], da.at[core], r["s_dar"].at[0], r["s_dar"].at[1], (sib, f))
-    dar.start()
-
-    dar.wait_recv()
-    for t in range(27):
-        r["gd"][t] = da[:, t].reshape(32, 128).astype(F32)
-    gd_copy = pltpu.make_async_copy(r["gd"], gd_out, r["s_out"].at[1])
-    gd_copy.start()
-
     def ear_copy(dj):
         piece = ea.at[core, lax.rem(j - dj + 8, 8)]
         return rcopy(piece, piece, r["s_ear"].at[0, dj], r["s_ear"].at[1, dj], (sib, f))
@@ -631,6 +655,18 @@
             ear_copy(dj).start()
             ea_copy(core, dj).start()
 
+    for k in range(1, 8):
+        from_j = lax.div(lax.rem(s + SPACE - 2 * k, SPACE), 2)
+        pl.when(from_j < OWNERS)(dag[k - 1].wait_recv)
+    dar = rcopy(da.at[core], da.at[core], r["s_dar"].at[0], r["s_dar"].at[1], (sib, f))
+    dar.start()
+
+    dar.wait_recv()
+    for t in range(27):
+        r["gd"][t] = da[:, t].reshape(32, 128).astype(F32)
+    gd_copy = pltpu.make_async_copy(r["gd"], gd_out, r["s_out"].at[1])
+    gd_copy.start()
+
     for dj in range(8):
 
         @pl.when(lax.rem(j - dj + 8, 8) < OWNERS)
@@ -638,9 +674,12 @@
             ear_copy(dj).wait_recv()
             ea_copy(other, dj).start()
 
-    for h in (halo_v, halo_p, halo_g):
+    for h in (halo_v, halo_p):
         h.wait_send()
-    for c in cots + wa + wb + wy + relay + pss + bos + gcs + [hcopy, dar]:
+    cot_all(0).wait_send()
+    pl.when(s > 0)(cot_all(1).wait_send)
+    pl.when(s < SPACE - 1)(cot_all(2).wait_send)
+    for c in wa + wb + wy + relay + pss + bos + gcs + [hcopy, dar]:
         c.wait_send()
     for copy, active in drs:
         pl.when(active)(copy.wait_send)

time: 65.3 us -> 62.3 us (0.954)
  Pallas kernels: 64.5 us -> 61.5 us
    pallas_call x1, Pallas kernels: 61.9 us -> 58.8 us  [shards(): pl.pallas_call(body, out_shape=(jax.ShapeDtypeStruct((16, 32, 64), BF), j...]
where the time goes in v3:
time: 62.3 us; the launch traced here: 62.1 us
  Pallas kernels  61.5 us (99%)
  between operations  0.64 us (1%)
    pallas_call x1, Pallas kernels, shards(): pl.pallas_call(body, out_shape=(jax.ShapeDtypeStruct((16, 32, 64), BF), j...  58.8 us
    pallas_call x1, Pallas kernels, shards(): pl.pallas_call(results, out_shape=(jax.ShapeDtypeStruct((16, 32, 64), BF)...  2.67 us

profile of v3, /device:TPU:1, one launch (start us, length us, event | category | flops | bytes accessed | tf_op | source)
XLA Modules:
  0.0 62.1 jit_solution(14906594886342382931)
XLA Ops:
  0.6 58.8 %step.1 = (bf16[16,32,64]{2,1,0:T(8,128)(2,1)}, bf16[2,7,8,8,512]{4,3,2,1,0:T(8,128)(2,1)}, f32[27,32,128]{2,1,0:T(8,128)}) custom-call(bf16[4,16,16,128]{3,2,1,0:T(8,128)(2,1)} %vol.1, bf16[9,384,128]{2,1,0:T(8,128)(2,1)} %bitcast.9, bf16[27,32,128]{2,1,0:T(8,128)(2,1)} %bitcast.10, bf16[16,32,64]{2,1,0:T(8,128)(2,1)} %bitcast.11), custom_call_target="tpu_custom_call" | custom-call | tf_op jit(solution)/shard_map/step/pallas_call | solution.py:749
  59.5 2.7 %results.1 = (bf16[16,32,64]{2,1,0:T(8,128)(2,1)}, f32[27,128,128]{2,1,0:T(8,128)}, f32[27,32,128]{2,1,0:T(8,128)}) custom-call(bf16[16,32,64]{2,1,0:T(8,128)(2,1)} %get-tuple-element.9.bo_in, bf16[2,7,8,8,512]{4,3,2,1,0:T(8,128)(2,1)} %get-tuple-element.10.ea_in, f32[27,32,128]{2,1,0:T(8,128)} %get-tuple-element.11.gd_in), custom_call_target="tpu_custom_call" | custom-call | tf_op jit(solution)/shard_map/results/pallas_call | solution.py:771

commit v4 on v3

--- a/solution.py
+++ b/solution.py
@@ -206,6 +206,11 @@
     def space_chip(k):
         return lax.rem(s + 2 * k, SPACE)
 
+    x_hi, z = lax.div(f, 4), lax.rem(f, 4)
+    near = s + 2 - 4 * lax.rem(j, 2)
+    w_to = [(s, 4 * x_hi + lax.rem(z + k, 4)) for k in range(1, 4)]
+    w_to += [(near, 4 * (1 - x_hi) + lax.rem(z + k, 4)) for k in range(4)]
+
     greeted = [(s, filt_peer(k)) for k in range(1, FILT)]
     greeted += [(space_chip(k), f) for k in range(1, 8)]
     greeted += [
@@ -213,6 +218,7 @@
         for d in (1, SPACE - 1)
         for df in range(FILT)
     ]
+    greeted += w_to[3:]
     for device in greeted:
         pl.semaphore_signal(barrier, inc=1, device_id=device, device_id_type=MESH)
 
@@ -273,7 +279,7 @@
             wg.at[taps, w_rows],
             r[sems].at[0, k],
             r[sems].at[1, k],
-            (s, filt_peer(k)),
+            w_to[k - 1],
         )
 
     for k in range(1, 8):
@@ -313,8 +319,6 @@
 
     r["cr"][1:3, :, pl.ds(f, 1)] = r["cs"][pl.ds(f, 1)].reshape(2, 2, 1, 16, 128)
 
-    own_vol.wait()
-    halo_v.wait_recv()
     for c in own_wd:
         c.wait()
     for c in wb:
@@ -331,6 +335,8 @@
         wy[-1].start()
     relay = [w_pass(share(y), "s_wrel", 0, (sib, f))]
     relay[-1].start()
+    own_vol.wait()
+    halo_v.wait_recv()
     zc = r["zc"]
     for row in range(6):
         x = r["vp"][row].astype(F32)

time: 62.3 us -> 60.8 us (0.976)
  Pallas kernels: 61.5 us -> 60 us
    pallas_call x1, Pallas kernels: 58.8 us -> 57.3 us  [shards(): pl.pallas_call(body, out_shape=(jax.ShapeDtypeStruct((16, 32, 64), BF), j...]
where the time goes in v4:
time: 60.8 us; the launch traced here: 60.6 us
  Pallas kernels  60 us (99%)
  between operations  0.64 us (1%)
    pallas_call x1, Pallas kernels, shards(): pl.pallas_call(body, out_shape=(jax.ShapeDtypeStruct((16, 32, 64), BF), j...  57.3 us
    pallas_call x1, Pallas kernels, shards(): pl.pallas_call(results, out_shape=(jax.ShapeDtypeStruct((16, 32, 64), BF)...  2.67 us

profile of v4, /device:TPU:1, one launch (start us, length us, event | category | flops | bytes accessed | tf_op | source)
XLA Modules:
  0.0 60.6 jit_solution(13537573159419115491)
XLA Ops:
  0.6 57.3 %step.1 = (bf16[16,32,64]{2,1,0:T(8,128)(2,1)}, bf16[2,7,8,8,512]{4,3,2,1,0:T(8,128)(2,1)}, f32[27,32,128]{2,1,0:T(8,128)}) custom-call(bf16[4,16,16,128]{3,2,1,0:T(8,128)(2,1)} %vol.1, bf16[9,384,128]{2,1,0:T(8,128)(2,1)} %bitcast.9, bf16[27,32,128]{2,1,0:T(8,128)(2,1)} %bitcast.10, bf16[16,32,64]{2,1,0:T(8,128)(2,1)} %bitcast.11), custom_call_target="tpu_custom_call" | custom-call | tf_op jit(solution)/shard_map/step/pallas_call | solution.py:755
  58.0 2.7 %results.1 = (bf16[16,32,64]{2,1,0:T(8,128)(2,1)}, f32[27,128,128]{2,1,0:T(8,128)}, f32[27,32,128]{2,1,0:T(8,128)}) custom-call(bf16[16,32,64]{2,1,0:T(8,128)(2,1)} %get-tuple-element.9.bo_in, bf16[2,7,8,8,512]{4,3,2,1,0:T(8,128)(2,1)} %get-tuple-element.10.ea_in, f32[27,32,128]{2,1,0:T(8,128)} %get-tuple-element.11.gd_in), custom_call_target="tpu_custom_call" | custom-call | tf_op jit(solution)/shard_map/results/pallas_call | solution.py:777

commit v5 on v4

--- a/solution.py
+++ b/solution.py
@@ -567,25 +567,6 @@
         bos[-1].start()
     r["br"][pl.ds(f, 1)] = r["bs"][:, pl.ds(f, 1)].reshape(1, 2, 16, 128)
 
-    ag_sends = []
-    for k in range(1, CHIPS):
-        piece = ea.at[core, jnp.minimum(j, OWNERS - 1), f]
-        device = (chips_s[k // 8], chips_f[k % 8])
-        ag_sends.append(rcopy(piece, piece, r["s_ag"].at[0], r["r_ag"].at[k // 8], device))
-
-    @pl.when(owner)
-    def _():
-        er[0] = es[0, pl.ds(f, 1)].reshape(8, 512)
-        landed = er.at[1:CHIPS]
-        rcopy(landed, landed, r["s_rs"].at[0], r["r_rs"].at[0], (s, f)).wait_recv()
-        total = jnp.sum(er[0:8].astype(F32), axis=0)
-        for n in range(1, 8):
-            total = total + jnp.sum(er[8 * n : 8 * n + 8].astype(F32), axis=0)
-        total = (total * early_scale).astype(BF).reshape(1, 1, 1, 8, 512)
-        ea[pl.ds(core, 1), pl.ds(j, 1), pl.ds(f, 1)] = total
-        for c in ag_sends:
-            c.start()
-
     hcopy.wait_recv()
     dsd = r["dsd"]
     dsd[27:28] = jnp.zeros((1, 16, 128), BF)
@@ -612,6 +593,25 @@
         drs.append((copy, to_j < OWNERS))
 
     mine_t = pl.ds(first_of(j), GROUP)
+
+    ag_sends = []
+    for k in range(1, CHIPS):
+        piece = ea.at[core, jnp.minimum(j, OWNERS - 1), f]
+        device = (chips_s[k // 8], chips_f[k % 8])
+        ag_sends.append(rcopy(piece, piece, r["s_ag"].at[0], r["r_ag"].at[k // 8], device))
+
+    @pl.when(owner)
+    def _():
+        er[0] = es[0, pl.ds(f, 1)].reshape(8, 512)
+        landed = er.at[1:CHIPS]
+        rcopy(landed, landed, r["s_rs"].at[0], r["r_rs"].at[0], (s, f)).wait_recv()
+        total = jnp.sum(er[0:8].astype(F32), axis=0)
+        for n in range(1, 8):
+            total = total + jnp.sum(er[8 * n : 8 * n + 8].astype(F32), axis=0)
+        total = (total * early_scale).astype(BF).reshape(1, 1, 1, 8, 512)
+        ea[pl.ds(core, 1), pl.ds(j, 1), pl.ds(f, 1)] = total
+        for c in ag_sends:
+            c.start()
 
     for c in bos:
         c.wait_recv()

time: 60.8 us -> 57.9 us (0.952)
  Pallas kernels: 60 us -> 57.1 us
    pallas_call x1, Pallas kernels: 57.3 us -> 54.5 us  [shards(): pl.pallas_call(body, out_shape=(jax.ShapeDtypeStruct((16, 32, 64), BF), j...]
where the time goes in v5:
time: 57.9 us; the launch traced here: 57.8 us
  Pallas kernels  57.1 us (99%)
  between operations  0.64 us (1%)
    pallas_call x1, Pallas kernels, shards(): pl.pallas_call(body, out_shape=(jax.ShapeDtypeStruct((16, 32, 64), BF), j...  54.5 us
    pallas_call x1, Pallas kernels, shards(): pl.pallas_call(results, out_shape=(jax.ShapeDtypeStruct((16, 32, 64), BF)...  2.67 us

profile of v5, /device:TPU:1, one launch (start us, length us, event | category | flops | bytes accessed | tf_op | source)
XLA Modules:
  0.0 57.8 jit_solution(3055397398471283899)
XLA Ops:
  0.6 54.5 %step.1 = (bf16[16,32,64]{2,1,0:T(8,128)(2,1)}, bf16[2,7,8,8,512]{4,3,2,1,0:T(8,128)(2,1)}, f32[27,32,128]{2,1,0:T(8,128)}) custom-call(bf16[4,16,16,128]{3,2,1,0:T(8,128)(2,1)} %vol.1, bf16[9,384,128]{2,1,0:T(8,128)(2,1)} %bitcast.9, bf16[27,32,128]{2,1,0:T(8,128)(2,1)} %bitcast.10, bf16[16,32,64]{2,1,0:T(8,128)(2,1)} %bitcast.11), custom_call_target="tpu_custom_call" | custom-call | tf_op jit(solution)/shard_map/step/pallas_call | solution.py:755
  55.1 2.7 %results.1 = (bf16[16,32,64]{2,1,0:T(8,128)(2,1)}, f32[27,128,128]{2,1,0:T(8,128)}, f32[27,32,128]{2,1,0:T(8,128)}) custom-call(bf16[16,32,64]{2,1,0:T(8,128)(2,1)} %get-tuple-element.9.bo_in, bf16[2,7,8,8,512]{4,3,2,1,0:T(8,128)(2,1)} %get-tuple-element.10.ea_in, f32[27,32,128]{2,1,0:T(8,128)} %get-tuple-element.11.gd_in), custom_call_target="tpu_custom_call" | custom-call | tf_op jit(solution)/shard_map/results/pallas_call | solution.py:777

commit v6 on v5

--- a/solution.py
+++ b/solution.py
@@ -644,6 +644,12 @@
         for c in dag:
             c.start()
 
+    for k in range(1, 8):
+        from_j = lax.div(lax.rem(s + SPACE - 2 * k, SPACE), 2)
+        pl.when(from_j < OWNERS)(dag[k - 1].wait_recv)
+    dar = rcopy(da.at[core], da.at[core], r["s_dar"].at[0], r["s_dar"].at[1], (sib, f))
+    dar.start()
+
     def ear_copy(dj):
         piece = ea.at[core, lax.rem(j - dj + 8, 8)]
         return rcopy(piece, piece, r["s_ear"].at[0, dj], r["s_ear"].at[1, dj], (sib, f))
@@ -660,12 +666,6 @@
             rcopy(landed, landed, r["s_ag"].at[0], r["r_ag"].at[dj], (s, f)).wait_recv()
             ear_copy(dj).start()
             ea_copy(core, dj).start()
-
-    for k in range(1, 8):
-        from_j = lax.div(lax.rem(s + SPACE - 2 * k, SPACE), 2)
-        pl.when(from_j < OWNERS)(dag[k - 1].wait_recv)
-    dar = rcopy(da.at[core], da.at[core], r["s_dar"].at[0], r["s_dar"].at[1], (sib, f))
-    dar.start()
 
     dar.wait_recv()
     for t in range(27):

time: 57.9 us -> 57.4 us (level)
  no operation moved by 1% of the time
where the time goes in v6:
time: 57.4 us; the launch traced here: 57.3 us
  Pallas kernels  56.7 us (99%)
  between operations  0.64 us (1%)
    pallas_call x1, Pallas kernels, shards(): pl.pallas_call(body, out_shape=(jax.ShapeDtypeStruct((16, 32, 64), BF), j...  54 us
    pallas_call x1, Pallas kernels, shards(): pl.pallas_call(results, out_shape=(jax.ShapeDtypeStruct((16, 32, 64), BF)...  2.67 us

profile of v6, /device:TPU:1, one launch (start us, length us, event | category | flops | bytes accessed | tf_op | source)
XLA Modules:
  0.0 57.3 jit_solution(10380411260599900820)
XLA Ops:
  0.6 54.0 %step.1 = (bf16[16,32,64]{2,1,0:T(8,128)(2,1)}, bf16[2,7,8,8,512]{4,3,2,1,0:T(8,128)(2,1)}, f32[27,32,128]{2,1,0:T(8,128)}) custom-call(bf16[4,16,16,128]{3,2,1,0:T(8,128)(2,1)} %vol.1, bf16[9,384,128]{2,1,0:T(8,128)(2,1)} %bitcast.9, bf16[27,32,128]{2,1,0:T(8,128)(2,1)} %bitcast.10, bf16[16,32,64]{2,1,0:T(8,128)(2,1)} %bitcast.11), custom_call_target="tpu_custom_call" | custom-call | tf_op jit(solution)/shard_map/step/pallas_call | solution.py:755
  54.6 2.7 %results.1 = (bf16[16,32,64]{2,1,0:T(8,128)(2,1)}, f32[27,128,128]{2,1,0:T(8,128)}, f32[27,32,128]{2,1,0:T(8,128)}) custom-call(bf16[16,32,64]{2,1,0:T(8,128)(2,1)} %get-tuple-element.9.bo_in, bf16[2,7,8,8,512]{4,3,2,1,0:T(8,128)(2,1)} %get-tuple-element.10.ea_in, f32[27,32,128]{2,1,0:T(8,128)} %get-tuple-element.11.gd_in), custom_call_target="tpu_custom_call" | custom-call | tf_op jit(solution)/shard_map/results/pallas_call | solution.py:777

commit v7 on v6

--- a/solution.py
+++ b/solution.py
@@ -613,6 +613,24 @@
         for c in ag_sends:
             c.start()
 
+    da = r["da"]
+    piece = da.at[core, mine_t]
+    dag = []
+    for k in range(1, 8):
+        dag.append(
+            rcopy(piece, piece, r["s_dag"].at[0, k], r["s_dag"].at[1, k], (space_chip(k), f))
+        )
+
+    @pl.when(owner)
+    def _():
+        total = dsd[mine_t].astype(F32)
+        for k in range(1, 8):
+            drs[k - 1][0].wait_recv()
+            total = total + r["dr"][k].astype(F32)
+        da[pl.ds(core, 1), mine_t] = (total * deep_scale).astype(BF).reshape(1, GROUP, 16, 128)
+        for c in dag:
+            c.start()
+
     for c in bos:
         c.wait_recv()
     parts = [jnp.zeros((32, 128), F32)] * 16
@@ -625,24 +643,6 @@
         r["bo"][p] = parts[p][:, 0:64].astype(BF)
     bo_copy = pltpu.make_async_copy(r["bo"], bo_out, r["s_out"].at[0])
     bo_copy.start()
-
-    da = r["da"]
-    piece = da.at[core, mine_t]
-    dag = []
-    for k in range(1, 8):
-        dag.append(
-            rcopy(piece, piece, r["s_dag"].at[0, k], r["s_dag"].at[1, k], (space_chip(k), f))
-        )
-
-    @pl.when(owner)
-    def _():
-        total = dsd[mine_t].astype(F32)
-        for k in range(1, 8):
-            drs[k - 1][0].wait_recv()
-            total = total + r["dr"][k].astype(F32)
-        da[pl.ds(core, 1), mine_t] = (total * deep_scale).astype(BF).reshape(1, GROUP, 16, 128)
-        for c in dag:
-            c.start()
 
     for k in range(1, 8):
         from_j = lax.div(lax.rem(s + SPACE - 2 * k, SPACE), 2)

time: 57.4 us -> 57.4 us (level)
  no operation moved by 1% of the time
where the time goes in v7:
time: 57.4 us; the launch traced here: 57.3 us
  Pallas kernels  56.7 us (99%)
  between operations  0.64 us (1%)
    pallas_call x1, Pallas kernels, shards(): pl.pallas_call(body, out_shape=(jax.ShapeDtypeStruct((16, 32, 64), BF), j...  54 us
    pallas_call x1, Pallas kernels, shards(): pl.pallas_call(results, out_shape=(jax.ShapeDtypeStruct((16, 32, 64), BF)...  2.67 us

profile of v7, /device:TPU:1, one launch (start us, length us, event | category | flops | bytes accessed | tf_op | source)
XLA Modules:
  0.0 57.3 jit_solution(6860251287202404235)
XLA Ops:
  0.6 54.0 %step.1 = (bf16[16,32,64]{2,1,0:T(8,128)(2,1)}, bf16[2,7,8,8,512]{4,3,2,1,0:T(8,128)(2,1)}, f32[27,32,128]{2,1,0:T(8,128)}) custom-call(bf16[4,16,16,128]{3,2,1,0:T(8,128)(2,1)} %vol.1, bf16[9,384,128]{2,1,0:T(8,128)(2,1)} %bitcast.9, bf16[27,32,128]{2,1,0:T(8,128)(2,1)} %bitcast.10, bf16[16,32,64]{2,1,0:T(8,128)(2,1)} %bitcast.11), custom_call_target="tpu_custom_call" | custom-call | tf_op jit(solution)/shard_map/step/pallas_call | solution.py:755
  54.6 2.7 %results.1 = (bf16[16,32,64]{2,1,0:T(8,128)(2,1)}, f32[27,128,128]{2,1,0:T(8,128)}, f32[27,32,128]{2,1,0:T(8,128)}) custom-call(bf16[16,32,64]{2,1,0:T(8,128)(2,1)} %get-tuple-element.9.bo_in, bf16[2,7,8,8,512]{4,3,2,1,0:T(8,128)(2,1)} %get-tuple-element.10.ea_in, f32[27,32,128]{2,1,0:T(8,128)} %get-tuple-element.11.gd_in), custom_call_target="tpu_custom_call" | custom-call | tf_op jit(solution)/shard_map/results/pallas_call | solution.py:777
